TPU v7x, 32 devices: a whole 2x2x4 slice. The times are simulated.
32 devices in a mesh: dp: 4 (over x, core), expert: 8 (over z, y).
Axes of the slice: x: 2, y: 2, z: 4, core: 2. Of those that a mesh axis runs over, the one named last changes fastest.
Arguments:
- tokens: bfloat16 [4096, 4096], P(('dp', 'expert')), may hold values from -6 to 6
- expert_ids: int32 [4096, 2], P(('dp', 'expert')), may hold values from 0 to 7, as said below
- gate_codes: int32 [4096, 2], P(('dp', 'expert')), may hold values from 1 to 64
- w_gate: bfloat16 [8, 4096, 768], P('expert'), may hold values from -0.09375 to 0.09375
- w_up: bfloat16 [8, 4096, 768], P('expert'), may hold values from -0.09375 to 0.09375
- w_down: bfloat16 [8, 768, 4096], P('expert'), may hold values from -0.21875 to 0.21875
- out_grad: bfloat16 [4096, 4096], P(('dp', 'expert')), may hold values from -6 to 6
Outputs:
- layer_out: bfloat16 [4096, 4096], P(('dp', 'expert'))
- tokens_grad: bfloat16 [4096, 4096], P(('dp', 'expert'))
- gate_weight_grad: bfloat16 [8, 4096, 768], P('expert', 'dp')
- up_weight_grad: bfloat16 [8, 4096, 768], P('expert', 'dp')
- down_weight_grad: bfloat16 [8, 768, 4096], P('expert', None, 'dp')
Inputs may be any that keep to these rules, and one draw needn't show every extreme that they name: `expert_ids`: each token names 2 different experts. In the rows of one device no expert is named more than 48 times, and in every draw one and the same expert is named exactly 48 times by the rows of every device.
All inputs are finite; a program needn't handle non-finite values.
Results may differ from a plain program's by a relative error of at most 0.009.
Values may be sent and summed in bfloat16 or wider, within the bound.
A program may use at most 192 MiB of HBM per device.

v0:
```python
import jax
import jax.numpy as jnp
from jax import lax
from jax.sharding import PartitionSpec as P


def slot_targets(block_ids, experts, capacity):
    flat_ids = block_ids.reshape(-1)
    one_hot = (flat_ids[:, None] == jnp.arange(experts, dtype=jnp.int32)[None, :]).astype(jnp.int32)
    earlier = jnp.cumsum(one_hot, axis=0) - one_hot
    slot_ranks = jnp.sum(earlier * one_hot, axis=1)
    return flat_ids * capacity + slot_ranks


def per_device(tokens, expert_ids, gate_codes, w_gate, w_up, w_down, out_grad):
    experts = lax.axis_size("expert")
    tok_count, model_width = tokens.shape
    top_count = expert_ids.shape[1]
    pair_count = tok_count * top_count
    capacity = 3 * pair_count // (2 * experts)
    targets = slot_targets(expert_ids, experts, capacity)
    owners = (
        jnp.full((experts * capacity,), -1, jnp.int32)
        .at[targets]
        .set(jnp.arange(pair_count, dtype=jnp.int32))
    )
    is_live = owners >= 0
    safe_pair = jnp.maximum(owners, 0)
    token_pos = safe_pair // top_count
    gate_flat = gate_codes.astype(jnp.float32).reshape(-1) / 64.0
    pair_gains = jnp.where(is_live, gate_flat[safe_pair], 0.0)
    outbound = jnp.where(is_live[:, None], tokens[token_pos], jnp.zeros((), jnp.bfloat16))
    outbound = outbound.reshape(experts, capacity, model_width)
    gate_matrix = w_gate[0]
    up_matrix = w_up[0]
    down_matrix = w_down[0]
    hidden_units = gate_matrix.shape[1]
    contract = (((1,), (1,)), ((), ()))
    contract_rows = (((0,), (0,)), ((), ()))
    received = lax.all_to_all(outbound, "expert", split_axis=0, concat_axis=0, tiled=True)
    slot_count = received.shape[1]
    expert_row_block = received.reshape(-1, model_width)
    pre_gate = jnp.dot(expert_row_block, gate_matrix, preferred_element_type=jnp.float32)
    pre_up = jnp.dot(expert_row_block, up_matrix, preferred_element_type=jnp.float32)
    expert_hidden = (pre_gate * jax.nn.sigmoid(pre_gate) * pre_up).astype(jnp.bfloat16)
    produced = jnp.dot(expert_hidden, down_matrix, preferred_element_type=jnp.float32).astype(
        jnp.bfloat16
    )
    produced = produced.reshape(experts, slot_count, model_width)
    returned = lax.all_to_all(produced, "expert", split_axis=0, concat_axis=0, tiled=True)
    returned, arrived, pre_gate, pre_up, hidden = (
        returned,
        received,
        pre_gate.reshape(experts, slot_count, hidden_units),
        pre_up.reshape(experts, slot_count, hidden_units),
        expert_hidden.reshape(experts, slot_count, hidden_units),
    )
    pair_out = returned.reshape(-1, model_width)[targets].astype(jnp.float32)
    weighted = gate_flat[:, None] * pair_out
    layer_out = jnp.sum(weighted.reshape(tok_count, top_count, model_width), axis=1).astype(
        jnp.bfloat16
    )
    upstream = out_grad[token_pos]
    pair_grad = (pair_gains[:, None] * upstream.astype(jnp.float32)).astype(jnp.bfloat16)
    pair_grad = pair_grad.reshape(experts, capacity, model_width)
    incoming = lax.all_to_all(pair_grad, "expert", split_axis=0, concat_axis=0, tiled=True).reshape(
        -1, model_width
    )
    pre_gate = pre_gate.reshape(-1, hidden_units)
    pre_up = pre_up.reshape(-1, hidden_units)
    hidden = hidden.reshape(-1, hidden_units)
    sigmoid_gate = jax.nn.sigmoid(pre_gate)
    silu_gate = pre_gate * sigmoid_gate
    hidden_grad = lax.dot_general(
        incoming, down_matrix, contract, preferred_element_type=jnp.float32
    )
    gate_pre_grad = (
        hidden_grad * pre_up * sigmoid_gate * (1.0 + pre_gate * (1.0 - sigmoid_gate))
    ).astype(jnp.bfloat16)
    up_pre_grad = (hidden_grad * silu_gate).astype(jnp.bfloat16)
    input_grad = lax.dot_general(
        gate_pre_grad, gate_matrix, contract, preferred_element_type=jnp.float32
    )
    input_grad = input_grad + lax.dot_general(
        up_pre_grad, up_matrix, contract, preferred_element_type=jnp.float32
    )
    input_grad = input_grad.astype(jnp.bfloat16).reshape(experts, capacity, model_width)
    returned_grad = lax.all_to_all(input_grad, "expert", split_axis=0, concat_axis=0, tiled=True)
    pair_input = returned_grad.reshape(-1, model_width)[targets].astype(jnp.float32)
    tokens_grad = jnp.sum(pair_input.reshape(tok_count, top_count, model_width), axis=1).astype(
        jnp.bfloat16
    )
    row_block = arrived.reshape(-1, model_width)
    column_block = row_block
    gate_sum = lax.psum_scatter(
        lax.dot_general(
            column_block, gate_pre_grad, contract_rows, preferred_element_type=jnp.float32
        ).astype(jnp.bfloat16),
        "dp",
        scatter_dimension=0,
        tiled=True,
    )
    column_block = row_block
    up_sum = lax.psum_scatter(
        lax.dot_general(
            column_block, up_pre_grad, contract_rows, preferred_element_type=jnp.float32
        ).astype(jnp.bfloat16),
        "dp",
        scatter_dimension=0,
        tiled=True,
    )
    column_block = incoming
    down_sum = (
        lax.psum_scatter(
            lax.dot_general(
                column_block, hidden, contract_rows, preferred_element_type=jnp.float32
            ).astype(jnp.bfloat16),
            "dp",
            scatter_dimension=0,
            tiled=True,
        )
        .astype(jnp.float32)
        .T
    )
    return (
        layer_out,
        tokens_grad,
        gate_sum[None],
        up_sum[None],
        down_sum.astype(jnp.bfloat16)[None],
    )


def solution(mesh):
    placed = (
        P(("dp", "expert"), None),
        P(("dp", "expert"), None),
        P(("dp", "expert"), None),
        P("expert", None, None),
        P("expert", None, None),
        P("expert", None, None),
        P(("dp", "expert"), None),
    )
    return jax.shard_map(
        per_device,
        mesh=mesh,
        in_specs=placed,
        out_specs=(
            P(("dp", "expert"), None),
            P(("dp", "expert"), None),
            P("expert", "dp", None),
            P("expert", "dp", None),
            P("expert", None, "dp"),
        ),
        check_vma=False,
    )
```

profile of v0, /device:TPU:0, one launch (start us, length us, event | category | flops | bytes accessed | tf_op | source)
XLA Modules:
  0.0 404.8 jit_solution(15272280271444568787)
XLA Ops:
  7.2 0.0 copy-start
  7.2 0.8 broadcast_multiply_fusion
  8.0 0.8 copy.16
  8.7 0.1 eq.29
  8.9 0.1 eq.25
  9.0 0.7 convert_multiply_fusion.1
  9.7 0.1 copy.14
  9.8 0.1 div.22
  10.0 0.1 copy.15
  10.1 0.1 mul.64
  10.2 0.6 reduce-window.6
  10.8 0.2 slice_reduce_fusion
  11.1 0.1 fusion.20
  11.2 1.4 scatter_custom_fusion
  12.6 2.8 gather_fusion.2
  15.5 0.1 mul.69
  15.5 0.0 copy-done
  15.5 4.1 %gather_fusion.3 = bf16[384,4096]{1,0:T(8,128)(2,1)} fusion(bf16[128,4096]{1,0:T(8,128)(2,1)S(1)} %copy-done, s32[1024]{0:T(1024)S(1)} %get-tuple-element.23), kind=kCustom, calls=%fused_computation.3 | custom fusion | bytes 6292992 | tf_op jit(solution)/shard_map/gather | solution.py:63
  19.6 4.6 %fusion = bf16[8,48,4096]{2,1,0:T(8,128)(2,1)} fusion(bf16[8,48,4096]{2,1,0:T(8,128)(2,1)} %bitcast.60, f32[8,48]{1,0:T(8,128)S(1)} %mul.69), kind=kLoop, calls=%fused_computation.10 | loop fusion | flops 4718592 | bytes 6292992 | tf_op jit(solution)/shard_map/convert_element_type | solution.py:64
  24.2 0.0 copy-start.2
  24.2 7.4 %all-to-all-start.2 = ((bf16[8,48,4096]{2,1,0:T(8,128)(2,1)}), bf16[8,48,4096]{2,1,0:T(8,128)(2,1)}, u32[]{:S(2)}, u32[]{:S(2)}) async-start(bf16[8,48,4096]{2,1,0:T(8,128)(2,1)} %fusion), calls=%async_computation.2 | async-start | bytes 6291456 | tf_op jit(solution)/shard_map/all_to_all | solution.py:66
  31.6 0.1 broadcast_in_dim.45
  31.7 0.0 copy-done.2
  31.7 4.0 gather_fusion
  35.7 3.9 broadcast_select_fusion
  39.6 62.8 %all-to-all-done.2 = bf16[8,48,4096]{2,1,0:T(8,128)(2,1)} async-done(((bf16[8,48,4096]{2,1,0:T(8,128)(2,1)}), bf16[8,48,4096]{2,1,0:T(8,128)(2,1)}, u32[]{:S(2)}, u32[]{:S(2)}) %all-to-all-start.2) | async-done | bytes 3145760 | tf_op jit(solution)/shard_map/all_to_all | solution.py:66
  102.4 3.6 all-to-all-start
  106.1 0.2 reduce-scatter.8.cloned.1.call-start
  106.3 7.4 %fusion.1 = f32[384,768]{1,0:T(8,128)} fusion(bf16[384,4096]{1,0:T(8,128)(2,1)} %bitcast.12, bf16[1,768,4096]{2,1,0:T(8,128)(2,1)} %param.12), kind=kOutput, calls=%fused_computation.11 | convolution fusion | flops 2415919104 | bytes 10616832 | tf_op jit(solution)/shard_map/dot_general | solution.py:74
  113.7 63.3 %all-to-all-done = bf16[8,48,4096]{2,1,0:T(8,128)(2,1)S(1)} async-done(((bf16[8,48,4096]{2,1,0:T(8,128)(2,1)}), bf16[8,48,4096]{2,1,0:T(8,128)(2,1)S(1)}, u32[]{:S(2)}, u32[]{:S(2)}) %all-to-all-start) | async-done | bytes 3145760 | tf_op jit(solution)/shard_map/all_to_all | solution.py:40
  176.9 0.0 copy-start.6
  176.9 5.5 %fusion.7 = f32[384,768]{1,0:T(8,128)S(1)} fusion(bf16[384,4096]{1,0:T(8,128)(2,1)S(1)} %bitcast.61, bf16[1,4096,768]{2,1,0:T(8,128)(2,1)} %param.11), kind=kOutput, calls=%fused_computation.17 | convolution fusion | flops 2415919104 | bytes 10616832 | tf_op jit(solution)/shard_map/dot_general | solution.py:44
  182.4 0.0 copy-done.6
  182.4 6.8 %multiply_convert_fusion.1 = (bf16[384,768]{1,0:T(8,128)(2,1)}, bf16[384,768]{1,0:T(8,128)(2,1)}, bf16[384,768]{1,0:T(8,128)(2,1)S(1)}) fusion(f32[384,768]{1,0:T(8,128)S(1)} %copy-done.6, f32[384,768]{1,0:T(8,128)S(1)} %fusion.7, bf16[384,4096]{1,0:T(8,128)(2,1)S(1)} %bitcast.62, bf16[1,4096,768]{2,1,0:T(8,128)(2,1)} %param.10), kind=kOutput, calls=%fused_computation.28 | convolution fusion | flops 2420342784 | bytes 13565952 | tf_op jit(solution)/shard_map/dot_general | solution.py:43
  189.2 0.0 copy-start.4
  189.2 0.8 copy-done.4
  190.0 8.0 %convolution_convert_fusion = bf16[4096,768]{1,0:T(8,128)(2,1)} fusion(bf16[384,4096]{1,0:T(8,128)(2,1)} %bitcast.12, bf16[384,768]{1,0:T(8,128)(2,1)S(1)} %get-tuple-element.19), kind=kOutput, calls=%fused_computation.6 | convolution fusion | flops 2419064832 | bytes 10027008 | tf_op jit(solution)/shard_map/dot_general | solution.py:115
  198.0 0.0 reduce-scatter.8.cloned.1.call-update
  198.1 0.0 reduce-scatter.4.cloned.1.call-start
  198.1 6.4 %convolution_convert_fusion.2 = bf16[4096,768]{1,0:T(8,128)(2,1)} fusion(bf16[384,4096]{1,0:T(8,128)(2,1)S(1)} %bitcast.63, bf16[384,768]{1,0:T(8,128)(2,1)} %get-tuple-element.17), kind=kOutput, calls=%fused_computation.8 | convolution fusion | flops 2419064832 | bytes 10027008 | tf_op jit(solution)/shard_map/dot_general | solution.py:96
  204.5 0.0 reduce-scatter.4.cloned.1.call-update
  204.5 0.3 reduce-scatter.6.cloned.1.call-start
  204.8 6.7 %convolution_convert_fusion.1 = bf16[4096,768]{1,0:T(8,128)(2,1)} fusion(bf16[384,4096]{1,0:T(8,128)(2,1)S(1)} %bitcast.64, bf16[384,768]{1,0:T(8,128)(2,1)} %get-tuple-element.18), kind=kOutput, calls=%fused_computation.7 | convolution fusion | flops 2419064832 | bytes 10027008 | tf_op jit(solution)/shard_map/dot_general | solution.py:105
  211.5 0.0 copy-start.5
  211.5 0.0 reduce-scatter.6.cloned.1.call-update
  211.5 1.0 copy-done.5
  212.5 6.8 %fusion.15 = bf16[384,4096]{1,0:T(8,128)(2,1)} fusion(bf16[384,768]{1,0:T(8,128)(2,1)S(1)} %copy-done.5, bf16[1,768,4096]{2,1,0:T(8,128)(2,1)} %param.12), kind=kOutput, calls=%fused_computation.24 | convolution fusion | flops 2417491968 | bytes 10027008 | tf_op jit(solution)/shard_map/dot_general | solution.py:46
  219.3 3.7 all-to-all-start.1
  223.0 0.0 copy-start.3
  223.0 4.9 %fusion.5 = f32[384,4096]{1,0:T(8,128)S(1)} fusion(bf16[384,768]{1,0:T(8,128)(2,1)} %get-tuple-element.18, bf16[1,4096,768]{2,1,0:T(8,128)(2,1)} %param.11), kind=kOutput, calls=%fused_computation.15 | convolution fusion | flops 2415919104 | bytes 13172736 | tf_op jit(solution)/shard_map/dot_general | solution.py:84
  228.0 0.0 copy-done.3
  228.0 8.5 %add_convert_fusion = bf16[384,4096]{1,0:T(8,128)(2,1)} fusion(f32[384,4096]{1,0:T(8,128)S(1)} %fusion.5, bf16[384,768]{1,0:T(8,128)(2,1)S(1)} %copy-done.3, bf16[1,4096,768]{2,1,0:T(8,128)(2,1)} %param.10), kind=kOutput, calls=%fused_computation.23 | convolution fusion | flops 2419064832 | bytes 16318464 | tf_op jit(solution)/shard_map/dot_general | solution.py:81
  236.5 57.5 %all-to-all-done.1 = bf16[8,48,4096]{2,1,0:T(8,128)(2,1)S(1)} async-done(((bf16[8,48,4096]{2,1,0:T(8,128)(2,1)}), bf16[8,48,4096]{2,1,0:T(8,128)(2,1)S(1)}, u32[]{:S(2)}, u32[]{:S(2)}) %all-to-all-start.1) | async-done | bytes 3145760 | tf_op jit(solution)/shard_map/all_to_all | solution.py:50
  294.0 4.4 %all-to-all-start.3 = ((bf16[8,48,4096]{2,1,0:T(8,128)(2,1)}), bf16[8,48,4096]{2,1,0:T(8,128)(2,1)}, u32[]{:S(2)}, u32[]{:S(2)}) async-start(bf16[8,48,4096]{2,1,0:T(8,128)(2,1)} %bitcast.65), calls=%async_computation.3 | async-start | bytes 6291456 | tf_op jit(solution)/shard_map/all_to_all | solution.py:88
  298.5 3.2 gather_fusion.1
  301.7 5.5 %reshape.118 = f32[128,2,4096]{2,1,0:T(2,128)} reshape(bf16[256,4096]{1,0:T(8,128)(2,1)} %gather_fusion.1) | data formatting | bytes 6291456 | tf_op jit(solution)/shard_map/convert_element_type | solution.py:58
  307.1 61.5 %all-to-all-done.3 = bf16[8,48,4096]{2,1,0:T(8,128)(2,1)} async-done(((bf16[8,48,4096]{2,1,0:T(8,128)(2,1)}), bf16[8,48,4096]{2,1,0:T(8,128)(2,1)}, u32[]{:S(2)}, u32[]{:S(2)}) %all-to-all-start.3) | async-done | bytes 3145760 | tf_op jit(solution)/shard_map/all_to_all | solution.py:88
  368.6 6.2 %gather_fusion.4 = bf16[256,4096]{1,0:T(8,128)(2,1)S(1)} fusion(bf16[384,4096]{1,0:T(8,128)(2,1)} %bitcast.14, s32[1024]{0:T(1024)S(1)} %pad_clamp_fusion.1), kind=kCustom, calls=%fused_computation.4 | custom fusion | bytes 4195328 | tf_op jit(solution)/shard_map/gather | solution.py:89
  374.8 2.9 gather.25
  377.7 0.0 copy-start.1
  377.7 7.9 %reduce_sum.35 = bf16[128,4096]{1,0:T(8,128)(2,1)} reduce(bf16[128,2,4096]{2,1,0:T(2,128)(2,1)} %gather.25, bf16[]{:T(256)} %constant.39.clone.1), dimensions={1}, to_apply=%region_5.6 | reduce | flops 524288 | bytes 3145730 | tf_op jit(solution)/shard_map/reduce_sum | solution.py:90
  385.6 9.6 %multiply_reduce_fusion = bf16[128,4096]{1,0:T(8,128)(2,1)} fusion(f32[128,2,4096]{2,1,0:T(2,128)} %reshape.118, f32[128,2]{1,0:T(8,128)S(1)} %copy.14), kind=kLoop, calls=%fused_computation.25 | loop fusion | flops 1572864 | bytes 5243904 | tf_op jit(solution)/shard_map/reduce_sum | solution.py:60
  395.3 2.6 copy.19
  397.9 0.0 copy-done.1
  (12 shorter events, 0.1 us)
Async XLA Ops:
  7.2 8.4 %copy-start = (bf16[128,4096]{1,0:T(8,128)(2,1)S(1)}, bf16[128,4096]{1,0:T(8,128)(2,1)}, u32[]{:S(2)}) copy-start(bf16[128,4096]{1,0:T(8,128)(2,1)} %param.13) | copy-start | bytes 3145732
  24.2 7.5 %copy-start.2 = (bf16[128,4096]{1,0:T(8,128)(2,1)S(1)}, bf16[128,4096]{1,0:T(8,128)(2,1)}, u32[]{:S(2)}) copy-start(bf16[128,4096]{1,0:T(8,128)(2,1)} %param.7) | copy-start | bytes 3145732
  24.2 78.2 %all-to-all-start.2 = ((bf16[8,48,4096]{2,1,0:T(8,128)(2,1)}), bf16[8,48,4096]{2,1,0:T(8,128)(2,1)}, u32[]{:S(2)}, u32[]{:S(2)}) async-start(bf16[8,48,4096]{2,1,0:T(8,128)(2,1)} %fusion), calls=%async_computation.2 | async-start | bytes 6291456 | tf_op jit(solution)/shard_map/all_to_all | solution.py:66
  102.4 74.5 %all-to-all-start = ((bf16[8,48,4096]{2,1,0:T(8,128)(2,1)}), bf16[8,48,4096]{2,1,0:T(8,128)(2,1)S(1)}, u32[]{:S(2)}, u32[]{:S(2)}) async-start(bf16[8,48,4096]{2,1,0:T(8,128)(2,1)} %broadcast_select_fusion), calls=%async_computation | async-start | bytes 6291456 | tf_op jit(solution)/shard_map/all_to_all | solution.py:40
  106.1 289.2 %reduce-scatter.8.cloned.1.call-start = ((), (), s32[]{:S(2)}) async-start(), calls=%async_computation.9 | async-start | bytes 7864320 | tf_op jit(solution)/shard_map/reduce_scatter | solution.py:114
  176.9 5.5 %copy-start.6 = (f32[384,768]{1,0:T(8,128)S(1)}, f32[384,768]{1,0:T(8,128)}, u32[]{:S(2)}) copy-start(f32[384,768]{1,0:T(8,128)} %fusion.1) | copy-start | bytes 3538948
  189.2 0.8 copy-start.4
  198.1 199.8 %reduce-scatter.4.cloned.1.call-start = ((), (), s32[]{:S(2)}) async-start(), calls=%async_computation.7 | async-start | bytes 7864320 | tf_op jit(solution)/shard_map/reduce_scatter | solution.py:95
  204.5 193.3 %reduce-scatter.6.cloned.1.call-start = ((), (), s32[]{:S(2)}) async-start(), calls=%async_computation.8 | async-start | bytes 7864320 | tf_op jit(solution)/shard_map/reduce_scatter | solution.py:104
  211.5 1.1 copy-start.5
  219.3 74.7 %all-to-all-start.1 = ((bf16[8,48,4096]{2,1,0:T(8,128)(2,1)}), bf16[8,48,4096]{2,1,0:T(8,128)(2,1)S(1)}, u32[]{:S(2)}, u32[]{:S(2)}) async-start(bf16[8,48,4096]{2,1,0:T(8,128)(2,1)} %bitcast.66), calls=%async_computation.1 | async-start | bytes 6291456 | tf_op jit(solution)/shard_map/all_to_all | solution.py:50
  223.0 5.0 %copy-start.3 = (bf16[384,768]{1,0:T(8,128)(2,1)S(1)}, bf16[384,768]{1,0:T(8,128)(2,1)}, u32[]{:S(2)}) copy-start(bf16[384,768]{1,0:T(8,128)(2,1)} %get-tuple-element.17) | copy-start | bytes 1769476
  294.0 74.6 %all-to-all-start.3 = ((bf16[8,48,4096]{2,1,0:T(8,128)(2,1)}), bf16[8,48,4096]{2,1,0:T(8,128)(2,1)}, u32[]{:S(2)}, u32[]{:S(2)}) async-start(bf16[8,48,4096]{2,1,0:T(8,128)(2,1)} %bitcast.65), calls=%async_computation.3 | async-start | bytes 6291456 | tf_op jit(solution)/shard_map/all_to_all | solution.py:88
  377.7 20.1 %copy-start.1 = (bf16[128,4096]{1,0:T(8,128)(2,1)S(1)}, bf16[128,4096]{1,0:T(8,128)(2,1)}, u32[]{:S(2)}) copy-start(bf16[128,4096]{1,0:T(8,128)(2,1)} %param.13) | copy-start | bytes 3145732
Sparse Core Ops, SparseCore 0:
  198.2 57.4 reduce-scatter.7
  258.9 58.3 reduce-scatter.3
  320.5 58.3 reduce-scatter.5
where the time goes:
time: 411 us; the launch traced here: 405 us
  waiting for transfers between devices  245 us (60%)
  matrix products  61 us (15%)
  local copies, waits for them, and re-layouts  36.5 us (9%)
  other arithmetic  28.2 us (7%)
  starting transfers between devices  19.7 us (5%)
  between operations  14.4 us (4%)
    all_to_all x1, waiting for transfers between devices, per_device(): lax.all_to_all(outbound, 'expert', split_axis=0, concat_axis=0, tiled=True)  63.3 us
    all_to_all x1, waiting for transfers between devices, per_device(): lax.all_to_all(pair_grad, 'expert', split_axis=0, concat_axis=0, tiled=True)  62.8 us
    all_to_all x1, waiting for transfers between devices, per_device(): lax.all_to_all(input_grad, 'expert', split_axis=0, concat_axis=0, tiled=T...  61.5 us
    all_to_all x1, waiting for transfers between devices, per_device(): lax.all_to_all(produced, 'expert', split_axis=0, concat_axis=0, tiled=True)  57.5 us
    reduce_sum x1, other arithmetic, per_device(): jnp.sum(weighted.reshape(tok_count, top_count, model_width), axis=1)  9.64 us
    gather x2, local copies, waits for them, and re-layouts, per_device(): returned_grad.reshape(-1, model_width)[targets].astype(jnp.float32)  9.08 us
    dot_general x1, matrix products, per_device(): lax.dot_general(gate_pre_grad, gate_matrix, contract, preferred_element_t...  8.54 us
  transfers between devices with their start and end apart: 7, of which 4 were waited for; matrix products, arithmetic and copies ran while one was open for 21% of the time, Pallas kernels for 0%

commit v1 on v0

v1 whole, which is shorter than its diff:
```python
import jax
import jax.numpy as jnp
from jax import lax
from jax.sharding import PartitionSpec as P


def selection(expert_ids, gate_codes, experts, capacity):
    tok_count = expert_ids.shape[0]
    expert_range = jnp.arange(experts, dtype=jnp.int32)
    named = expert_ids[:, :, None] == expert_range[None, None, :]
    chosen = jnp.any(named, axis=1).T
    gates = jnp.sum(jnp.where(named, gate_codes[:, :, None], 0), axis=1).T
    gates = gates.astype(jnp.float32) * (1.0 / 64.0)
    earlier = (
        jnp.arange(tok_count, dtype=jnp.int32)[:, None] < jnp.arange(tok_count, dtype=jnp.int32)[None, :]
    )
    ranks = jnp.dot(
        chosen.astype(jnp.bfloat16), earlier.astype(jnp.bfloat16), preferred_element_type=jnp.float32
    ).astype(jnp.int32)
    slots = jnp.where(chosen, ranks, -1)
    hit = slots[:, None, :] == jnp.arange(capacity, dtype=jnp.int32)[None, :, None]
    sel = hit.astype(jnp.bfloat16).reshape(experts * capacity, tok_count)
    sel_gate = jnp.where(hit, gates[:, None, :], 0.0).astype(jnp.bfloat16)
    return sel, sel_gate.reshape(experts * capacity, tok_count)


def swap_columns(rows, groups, me):
    width = rows.shape[1] // groups
    parts = [lax.dynamic_slice_in_dim(rows, me * width, width, axis=1)]
    for shift in range(1, groups):
        target = lax.rem(me + shift, groups)
        piece = lax.dynamic_slice_in_dim(rows, target * width, width, axis=1)
        parts.append(
            lax.ppermute(piece, "dp", [(i, (i + shift) % groups) for i in range(groups)])
        )
    return parts


def per_device(tokens, expert_ids, gate_codes, w_gate, w_up, w_down, out_grad):
    experts = lax.axis_size("expert")
    groups = lax.axis_size("dp")
    me = lax.axis_index("dp")
    tok_count, model_width = tokens.shape
    pair_count = tok_count * expert_ids.shape[1]
    capacity = 3 * pair_count // (2 * experts)
    f32 = jnp.float32
    bf16 = jnp.bfloat16
    sel, sel_gate = selection(expert_ids, gate_codes, experts, capacity)
    gate_matrix, up_matrix, down_matrix = w_gate[0], w_up[0], w_down[0]
    hidden_units = gate_matrix.shape[1]
    contract = (((1,), (1,)), ((), ()))
    contract_rows = (((0,), (0,)), ((), ()))

    def exchange(rows):
        rows = rows.reshape(experts, capacity, model_width)
        rows = lax.all_to_all(rows, "expert", split_axis=0, concat_axis=0, tiled=True)
        return rows.reshape(experts * capacity, model_width)

    arrived = exchange(jnp.dot(sel, tokens, preferred_element_type=f32).astype(bf16))
    incoming = exchange(jnp.dot(sel_gate, out_grad, preferred_element_type=f32).astype(bf16))
    pre_gate = jnp.dot(arrived, gate_matrix, preferred_element_type=f32)
    pre_up = jnp.dot(arrived, up_matrix, preferred_element_type=f32)
    sigmoid_gate = jax.nn.sigmoid(pre_gate)
    silu_gate = pre_gate * sigmoid_gate
    hidden = (silu_gate * pre_up).astype(bf16)
    produced = jnp.dot(hidden, down_matrix, preferred_element_type=f32).astype(bf16)
    returned = exchange(produced)
    layer_out = lax.dot_general(sel_gate, returned, contract_rows, preferred_element_type=f32)

    arrived_parts = swap_columns(arrived, groups, me)
    incoming_parts = swap_columns(incoming, groups, me)

    hidden_grad = lax.dot_general(incoming, down_matrix, contract, preferred_element_type=f32)
    gate_pre_grad = (
        hidden_grad * pre_up * sigmoid_gate * (1.0 + pre_gate * (1.0 - sigmoid_gate))
    ).astype(bf16)
    up_pre_grad = (hidden_grad * silu_gate).astype(bf16)
    input_grad = lax.dot_general(gate_pre_grad, gate_matrix, contract, preferred_element_type=f32)
    input_grad = input_grad + lax.dot_general(
        up_pre_grad, up_matrix, contract, preferred_element_type=f32
    )
    returned_grad = exchange(input_grad.astype(bf16))
    tokens_grad = lax.dot_general(sel, returned_grad, contract_rows, preferred_element_type=f32)

    factors = jnp.concatenate([gate_pre_grad, up_pre_grad, hidden], axis=0)
    gathered = lax.all_gather(factors, "dp", axis=0, tiled=False)
    rows = experts * capacity

    gate_sum = up_sum = down_sum = 0.0
    for shift in range(groups):
        source = lax.rem(me - shift + groups, groups)
        factor = factors if shift == 0 else lax.dynamic_index_in_dim(gathered, source, 0, keepdims=False)
        tok, grad = arrived_parts[shift], incoming_parts[shift]
        gate_sum += lax.dot_general(tok, factor[:rows], contract_rows, preferred_element_type=f32)
        up_sum += lax.dot_general(
            tok, factor[rows : 2 * rows], contract_rows, preferred_element_type=f32
        )
        down_sum += lax.dot_general(
            factor[2 * rows :], grad, contract_rows, preferred_element_type=f32
        )
    return (
        layer_out.astype(bf16),
        tokens_grad.astype(bf16),
        gate_sum.astype(bf16)[None],
        up_sum.astype(bf16)[None],
        down_sum.astype(bf16)[None],
    )


def solution(mesh):
    placed = (
        P(("dp", "expert"), None),
        P(("dp", "expert"), None),
        P(("dp", "expert"), None),
        P("expert", None, None),
        P("expert", None, None),
        P("expert", None, None),
        P(("dp", "expert"), None),
    )
    return jax.shard_map(
        per_device,
        mesh=mesh,
        in_specs=placed,
        out_specs=(
            P(("dp", "expert"), None),
            P(("dp", "expert"), None),
            P("expert", "dp", None),
            P("expert", "dp", None),
            P("expert", None, "dp"),
        ),
        check_vma=False,
    )
```

time: 411 us -> 367 us (0.89); the launches traced: 405 us -> 366 us
  local copies, waits for them, and re-layouts: 36.5 us -> 5.87 us
  other arithmetic: 28.2 us -> 3.77 us
  matrix products: 61 us -> 82.9 us
  waiting for transfers between devices: 245 us -> 234 us
  starting transfers between devices: 19.7 us -> 24.8 us
    gather x6 -> x0, local copies, waits for them, and re-layouts: 23.2 us -> none  [the longest x2 9.08 us: per_device(): returned_grad.reshape(-1, model_width)[targets].astype(jnp.float32)]
    dot_general x7 -> x21, matrix products: 47.5 us -> 69.2 us  [the longest x4 11.9 us: per_device(): lax.dot_general(factor[2 * rows:], grad, contract_rows, preferred_element...]
    reduce_sum x3 -> x1, other arithmetic: 17.6 us -> 0.01 us  [selection(): gates = jnp.sum(jnp.where(named, gate_codes[:, :, None], 0), axis=1).T]
    all_to_all x4, waiting for transfers between devices: 245 us -> 234 us  [exchange(): lax.all_to_all(rows, 'expert', split_axis=0, concat_axis=0, tiled=True)]
    convert_element_type x1 -> x0, local copies, waits for them, and re-layouts: 5.47 us -> none  [per_device(): pair_out = returned.reshape(-1, model_width)[targets].astype(jnp.float32)]
    dynamic_slice x0 -> x2, local copies, waits for them, and re-layouts: none -> 4.64 us  [swap_columns(): piece = lax.dynamic_slice_in_dim(rows, target * width, width, axis=1)]
    convert_element_type x2 -> x1, other arithmetic: 4.57 us -> 0.12 us  [selection(): sel_gate = jnp.where(hit, gates[:, None, :], 0.0).astype(jnp.bfloat16)]
  transfers between devices with their start and end apart: 7 -> 11, of which waited for: 4 -> 4; matrix products, arithmetic and copies ran while one was open for 21% -> 18% of each run, Pallas kernels for 0% -> 0%
where the time goes in v1:
time: 367 us; the launch traced here: 366 us
  waiting for transfers between devices  234 us (64%)
  matrix products  82.9 us (23%)
  starting transfers between devices  24.8 us (7%)
  between operations  14.3 us (4%)
  local copies, waits for them, and re-layouts  5.87 us (2%)
  other arithmetic  3.77 us (1%)
    all_to_all x4, waiting for transfers between devices, exchange(): lax.all_to_all(rows, 'expert', split_axis=0, concat_axis=0, tiled=True)  234 us
    all_to_all x4, starting transfers between devices, exchange(): lax.all_to_all(rows, 'expert', split_axis=0, concat_axis=0, tiled=True)  20.8 us
    dot_general x4, matrix products, per_device(): lax.dot_general(factor[2 * rows:], grad, contract_rows, preferred_element...  11.9 us
    dot_general x4, matrix products, per_device(): lax.dot_general(tok, factor[:rows], contract_rows, preferred_element_type...  10.9 us
    dot_general x1, matrix products, per_device(): lax.dot_general(gate_pre_grad, gate_matrix, contract, preferred_element_t...  8.74 us
    dot_general x4, matrix products, per_device(): lax.dot_general(tok, factor[rows:2 * rows], contract_rows, preferred_elem...  8.68 us
  transfers between devices with their start and end apart: 11, of which 4 were waited for; matrix products, arithmetic and copies ran while one was open for 18% of the time, Pallas kernels for 0%

profile of v1, /device:TPU:0, one launch (start us, length us, event | category | flops | bytes accessed | tf_op | source)
XLA Modules:
  0.0 365.8 jit_solution(1978178762770404817)
XLA Ops:
  7.2 0.0 copy-start
  7.2 0.8 fusion.44
  8.0 0.1 fusion.23
  8.1 0.1 eq.46
  8.2 0.1 bitcast_compare_fusion
  8.3 0.1 copy-done
  8.4 2.6 convolution_convert_fusion.1
  11.0 7.4 %all-to-all-start = ((bf16[8,48,4096]{2,1,0:T(8,128)(2,1)}), bf16[8,48,4096]{2,1,0:T(8,128)(2,1)S(1)}, u32[]{:S(2)}, u32[]{:S(2)}) async-start(bf16[8,48,4096]{2,1,0:T(8,128)(2,1)} %bitcast.112), calls=%async_computation | async-start | bytes 6291456 | tf_op jit(solution)/shard_map/all_to_all | solution.py:56
  18.5 0.1 fusion.39
  18.6 3.8 %convolution_convert_fusion = bf16[384,4096]{1,0:T(8,128)(2,1)} fusion(bf16[384,128]{1,0:T(8,128)(2,1)S(1)} %fusion.39, bf16[128,4096]{1,0:T(8,128)(2,1)} %param.13), kind=kOutput, calls=%fused_computation.14 | convolution fusion | flops 404226048 | bytes 4292608 | tf_op jit(solution)/shard_map/dot_general | solution.py:60
  22.4 66.7 %all-to-all-done = bf16[8,48,4096]{2,1,0:T(8,128)(2,1)S(1)} async-done(((bf16[8,48,4096]{2,1,0:T(8,128)(2,1)}), bf16[8,48,4096]{2,1,0:T(8,128)(2,1)S(1)}, u32[]{:S(2)}, u32[]{:S(2)}) %all-to-all-start) | async-done | bytes 3145760 | tf_op jit(solution)/shard_map/all_to_all | solution.py:56
  89.1 4.5 %all-to-all-start.2 = ((bf16[8,48,4096]{2,1,0:T(8,128)(2,1)}), bf16[8,48,4096]{2,1,0:T(8,128)(2,1)}, u32[]{:S(2)}, u32[]{:S(2)}) async-start(bf16[8,48,4096]{2,1,0:T(8,128)(2,1)} %bitcast.11), calls=%async_computation.2 | async-start | bytes 6291456 | tf_op jit(solution)/shard_map/all_to_all | solution.py:56
  93.6 6.4 %fusion.6 = f32[384,768]{1,0:T(8,128)} fusion(bf16[384,4096]{1,0:T(8,128)(2,1)S(1)} %bitcast.113, bf16[1,4096,768]{2,1,0:T(8,128)(2,1)} %param.11), kind=kOutput, calls=%fused_computation.6 | convolution fusion | flops 2415919104 | bytes 10616832 | tf_op jit(solution)/shard_map/dot_general | solution.py:62
  100.0 63.8 %all-to-all-done.2 = bf16[8,48,4096]{2,1,0:T(8,128)(2,1)} async-done(((bf16[8,48,4096]{2,1,0:T(8,128)(2,1)}), bf16[8,48,4096]{2,1,0:T(8,128)(2,1)}, u32[]{:S(2)}, u32[]{:S(2)}) %all-to-all-start.2) | async-done | bytes 3145760 | tf_op jit(solution)/shard_map/all_to_all | solution.py:56
  163.8 6.5 %fusion = f32[384,768]{1,0:T(8,128)S(1)} fusion(bf16[384,4096]{1,0:T(8,128)(2,1)} %bitcast.12, bf16[1,768,4096]{2,1,0:T(8,128)(2,1)} %param.12), kind=kOutput, calls=%fused_computation | convolution fusion | flops 2415919104 | bytes 10616832 | tf_op jit(solution)/shard_map/dot_general | solution.py:73
  170.3 0.0 slice-start.1
  170.3 6.9 %multiply_convert_fusion.1 = (bf16[384,768]{1,0:T(8,128)(2,1)}, bf16[384,768]{1,0:T(8,128)(2,1)}, bf16[384,768]{1,0:T(8,128)(2,1)S(1)}) fusion(f32[384,768]{1,0:T(8,128)S(1)} %fusion, f32[384,768]{1,0:T(8,128)S(1)} %copy-done.14, bf16[384,4096]{1,0:T(8,128)(2,1)S(1)} %bitcast.114, bf16[1,4096,768]{2,1,0:T(8,128)(2,1)} %param.10), kind=kOutput, calls=%fused_computation.28 | convolution fusion | flops 2420342784 | bytes 13565952 | tf_op jit(solution)/shard_map/dot_general | solution.py:61
  177.3 4.1 %fusion.14 = bf16[384,4096]{1,0:T(8,128)(2,1)} fusion(bf16[384,768]{1,0:T(8,128)(2,1)S(1)} %get-tuple-element.13, bf16[1,768,4096]{2,1,0:T(8,128)(2,1)S(1)} %bitcast.130), kind=kOutput, calls=%fused_computation.13 | convolution fusion | flops 2417491968 | bytes 10027008 | tf_op jit(solution)/shard_map/dot_general | solution.py:66
  181.4 0.0 copy-done.6
  181.4 4.5 %all-to-all-start.1 = ((bf16[8,48,4096]{2,1,0:T(8,128)(2,1)}), bf16[8,48,4096]{2,1,0:T(8,128)(2,1)}, u32[]{:S(2)}, u32[]{:S(2)}) async-start(bf16[8,48,4096]{2,1,0:T(8,128)(2,1)} %bitcast.128), calls=%async_computation.1 | async-start | bytes 6291456 | tf_op jit(solution)/shard_map/all_to_all | solution.py:56
  185.8 0.2 all-gather.3.cloned.1.call-start
  186.1 2.7 pad_maximum_fusion
  188.8 0.0 all-gather.3.cloned.1.call-update
  188.8 0.0 copy-start.9
  188.9 5.0 %fusion.4 = f32[384,4096]{1,0:T(8,128)S(1)} fusion(bf16[384,768]{1,0:T(8,128)(2,1)} %get-tuple-element.12, bf16[1,4096,768]{2,1,0:T(8,128)(2,1)} %param.11), kind=kOutput, calls=%fused_computation.4 | convolution fusion | flops 2415919104 | bytes 13172736 | tf_op jit(solution)/shard_map/dot_general | solution.py:79
  193.8 8.7 %add_convert_fusion = bf16[384,4096]{1,0:T(8,128)(2,1)} fusion(f32[384,4096]{1,0:T(8,128)S(1)} %fusion.4, bf16[384,768]{1,0:T(8,128)(2,1)S(1)} %copy-done.9, bf16[1,4096,768]{2,1,0:T(8,128)(2,1)} %param.10), kind=kOutput, calls=%fused_computation.12 | convolution fusion | flops 2419064832 | bytes 16318464 | tf_op jit(solution)/shard_map/dot_general | solution.py:78
  202.6 53.5 %all-to-all-done.1 = bf16[8,48,4096]{2,1,0:T(8,128)(2,1)} async-done(((bf16[8,48,4096]{2,1,0:T(8,128)(2,1)}), bf16[8,48,4096]{2,1,0:T(8,128)(2,1)}, u32[]{:S(2)}, u32[]{:S(2)}) %all-to-all-start.1) | async-done | bytes 3145760 | tf_op jit(solution)/shard_map/all_to_all | solution.py:56
  256.0 4.5 %all-to-all-start.3 = ((bf16[8,48,4096]{2,1,0:T(8,128)(2,1)}), bf16[8,48,4096]{2,1,0:T(8,128)(2,1)}, u32[]{:S(2)}, u32[]{:S(2)}) async-start(bf16[8,48,4096]{2,1,0:T(8,128)(2,1)} %bitcast.127), calls=%async_computation.3 | async-start | bytes 6291456 | tf_op jit(solution)/shard_map/all_to_all | solution.py:56
  260.6 1.5 constant_dynamic-slice_fusion.3
  262.0 0.0 collective-permute-start
  262.0 0.0 copy-done.7
  262.1 4.0 %fusion.24 = f32[768,1024]{1,0:T(8,128)} fusion(bf16[384,768]{1,0:T(8,128)(2,1)S(1)} %copy-done.7, bf16[384,4096]{1,0:T(8,128)(2,1)} %bitcast.12, s32[]{:T(128)S(6)} %select_n.45), kind=kOutput, calls=%fused_computation.34 | convolution fusion | flops 603979776 | bytes 4521988 | tf_op jit(solution)/shard_map/dot_general | solution.py:98
  266.1 0.0 copy-done.11
  266.1 1.0 fusion.26
  267.1 0.0 copy-done.10
  267.2 2.8 fusion.28
  270.0 3.2 constant_dynamic-slice_fusion
  273.1 1.5 collective-permute-start.4
  274.6 0.2 collective-permute-start.3
  274.8 1.5 collective-permute-start.5
  276.3 0.5 collective-permute-start.1
  276.9 3.6 fusion.17
  280.5 50.2 %all-to-all-done.3 = bf16[8,48,4096]{2,1,0:T(8,128)(2,1)} async-done(((bf16[8,48,4096]{2,1,0:T(8,128)(2,1)}), bf16[8,48,4096]{2,1,0:T(8,128)(2,1)}, u32[]{:S(2)}, u32[]{:S(2)}) %all-to-all-start.3) | async-done | bytes 3145760 | tf_op jit(solution)/shard_map/all_to_all | solution.py:56
  330.6 3.6 fusion.18
  334.3 0.0 collective-permute-done
  334.3 0.0 collective-permute-start.2
  334.3 0.0 all-gather.3.cloned.1.call-done
  334.3 0.0 copy-start.8
  334.3 2.5 fusion.38
  336.8 0.9 copy-done.8
  337.7 2.1 fusion.35
  339.9 0.0 collective-permute-done.1
  339.9 2.2 fusion.34
  342.0 2.2 fusion.37
  344.2 0.0 collective-permute-done.4
  344.2 2.2 fusion.31
  346.4 0.0 collective-permute-done.2
  346.4 3.4 fusion.20
  349.8 0.0 collective-permute-done.3
  349.8 2.3 fusion.32
  352.1 0.0 copy-start.1
  352.1 3.5 fusion.19
  355.6 0.0 collective-permute-done.5
  355.6 3.4 fusion.21
  (27 shorter events, 0.1 us)
Async XLA Ops:
  7.2 1.2 copy-start
  11.0 7.4 %copy-start.12 = (s32[128,2]{0,1:T(2,128)S(1)}, s32[128,2]{0,1:T(2,128)}, u32[]{:S(2)}) copy-start(s32[128,2]{0,1:T(2,128)} %param.8) | copy-start | bytes 3076
  11.0 7.4 %copy-start.13 = (s32[128,2]{0,1:T(2,128)S(1)}, s32[128,2]{0,1:T(2,128)}, u32[]{:S(2)}) copy-start(s32[128,2]{0,1:T(2,128)} %param.9) | copy-start | bytes 3076
  11.0 78.1 %all-to-all-start = ((bf16[8,48,4096]{2,1,0:T(8,128)(2,1)}), bf16[8,48,4096]{2,1,0:T(8,128)(2,1)S(1)}, u32[]{:S(2)}, u32[]{:S(2)}) async-start(bf16[8,48,4096]{2,1,0:T(8,128)(2,1)} %bitcast.112), calls=%async_computation | async-start | bytes 6291456 | tf_op jit(solution)/shard_map/all_to_all | solution.py:56
  89.1 171.4 %copy-start.4 = (bf16[8,48,4096]{2,1,0:T(8,128)(2,1)}, bf16[8,48,4096]{2,1,0:T(8,128)(2,1)S(1)}, u32[]{:S(2)}) copy-start(bf16[8,48,4096]{2,1,0:T(8,128)(2,1)S(1)} %all-to-all-done) | copy-start | bytes 9437188
  89.1 74.6 %all-to-all-start.2 = ((bf16[8,48,4096]{2,1,0:T(8,128)(2,1)}), bf16[8,48,4096]{2,1,0:T(8,128)(2,1)}, u32[]{:S(2)}, u32[]{:S(2)}) async-start(bf16[8,48,4096]{2,1,0:T(8,128)(2,1)} %bitcast.11), calls=%async_computation.2 | async-start | bytes 6291456 | tf_op jit(solution)/shard_map/all_to_all | solution.py:56
  163.8 6.5 %copy-start.14 = (f32[384,768]{1,0:T(8,128)S(1)}, f32[384,768]{1,0:T(8,128)}, u32[]{:S(2)}) copy-start(f32[384,768]{1,0:T(8,128)} %fusion.6) | copy-start | bytes 3538948
  163.8 13.5 %slice-start = ((s8[6291456]{0:T(1024)(128)(4,1)}), s8[2097152]{0:T(1024)(128)(4,1)S(1)}, s32[]{:S(2)}) async-start(s8[6291456]{0:T(1024)(128)(4,1)} %bitcast.129), calls=%async_computation.5 | async-start | bytes 4194304
  170.3 7.0 %slice-start.1 = ((s8[6291456]{0:T(1024)(128)(4,1)}), s8[4194304]{0:T(1024)(128)(4,1)S(1)}, s32[]{:S(2)}) async-start(s8[6291456]{0:T(1024)(128)(4,1)} %bitcast.129), calls=%async_computation.6 | async-start | bytes 8388608
  177.3 4.1 %copy-start.6 = (bf16[384,768]{1,0:T(8,128)(2,1)}, bf16[384,768]{1,0:T(8,128)(2,1)S(1)}, u32[]{:S(2)}) copy-start(bf16[384,768]{1,0:T(8,128)(2,1)S(1)} %get-tuple-element.13) | copy-start | bytes 1769476
  181.4 74.6 %all-to-all-start.1 = ((bf16[8,48,4096]{2,1,0:T(8,128)(2,1)}), bf16[8,48,4096]{2,1,0:T(8,128)(2,1)}, u32[]{:S(2)}, u32[]{:S(2)}) async-start(bf16[8,48,4096]{2,1,0:T(8,128)(2,1)} %bitcast.128), calls=%async_computation.1 | async-start | bytes 6291456 | tf_op jit(solution)/shard_map/all_to_all | solution.py:56
  185.8 148.4 %all-gather.3.cloned.1.call-start = ((), (), s32[]{:S(2)}) async-start(), calls=%async_computation.4 | async-start | bytes 8847360 | tf_op jit(solution)/shard_map/all_gather | solution.py:86
  188.8 5.0 %copy-start.9 = (bf16[384,768]{1,0:T(8,128)(2,1)S(1)}, bf16[384,768]{1,0:T(8,128)(2,1)}, u32[]{:S(2)}) copy-start(bf16[384,768]{1,0:T(8,128)(2,1)} %get-tuple-element.11) | copy-start | bytes 1769476
  256.0 74.6 %all-to-all-start.3 = ((bf16[8,48,4096]{2,1,0:T(8,128)(2,1)}), bf16[8,48,4096]{2,1,0:T(8,128)(2,1)}, u32[]{:S(2)}, u32[]{:S(2)}) async-start(bf16[8,48,4096]{2,1,0:T(8,128)(2,1)} %bitcast.127), calls=%async_computation.3 | async-start | bytes 6291456 | tf_op jit(solution)/shard_map/all_to_all | solution.py:56
  260.5 1.5 copy-start.7
  262.0 4.1 %copy-start.5 = (bf16[8,48,4096]{2,1,0:T(8,128)(2,1)S(1)}, bf16[8,48,4096]{2,1,0:T(8,128)(2,1)}, u32[]{:S(2)}) copy-start(bf16[8,48,4096]{2,1,0:T(8,128)(2,1)} %copy-done.4) | copy-start | bytes 9437188
  262.0 4.1 %copy-start.11 = (bf16[384,768]{1,0:T(8,128)(2,1)S(1)}, bf16[384,768]{1,0:T(8,128)(2,1)}, u32[]{:S(2)}) copy-start(bf16[384,768]{1,0:T(8,128)(2,1)} %get-tuple-element.12) | copy-start | bytes 1769476
  262.0 72.2 %collective-permute-start = (bf16[384,1024]{1,0:T(8,128)(2,1)}, bf16[384,1024]{1,0:T(8,128)(2,1)}, u32[]{:S(2)}, u32[]{:S(2)}) collective-permute-start(bf16[384,1024]{1,0:T(8,128)(2,1)} %get-tuple-element.10), channel_id=1, source_target_pairs={{0,8},{8,16},{16,24},{24,0},{1,9},{9,17},{17,25},{25,1},{2,10},{10... | collective-permute-start | bytes 2359304 | tf_op jit(solution)/shard_map/ppermute | solution.py:34
  266.1 1.1 copy-start.10
  273.1 71.1 %collective-permute-start.4 = (bf16[384,1024]{1,0:T(8,128)(2,1)}, bf16[384,1024]{1,0:T(8,128)(2,1)}, u32[]{:S(2)}, u32[]{:S(2)}) collective-permute-start(bf16[384,1024]{1,0:T(8,128)(2,1)} %get-tuple-element.6), channel_id=1, source_target_pairs={{0,16},{8,24},{16,0},{24,8},{1,17},{9,25},{17,1},{25,9},{2,18},{10... | collective-permute-start | bytes 2359304 | tf_op jit(solution)/shard_map/ppermute | solution.py:34
  274.6 75.2 %collective-permute-start.3 = (bf16[384,1024]{1,0:T(8,128)(2,1)}, bf16[384,1024]{1,0:T(8,128)(2,1)}, u32[]{:S(2)}, u32[]{:S(2)}) collective-permute-start(bf16[384,1024]{1,0:T(8,128)(2,1)} %get-tuple-element.7), channel_id=1, source_target_pairs={{0,8},{8,16},{16,24},{24,0},{1,9},{9,17},{17,25},{25,1},{2,10},{10... | collective-permute-start | bytes 2359304 | tf_op jit(solution)/shard_map/ppermute | solution.py:34
  274.8 80.8 %collective-permute-start.5 = (bf16[384,1024]{1,0:T(8,128)(2,1)}, bf16[384,1024]{1,0:T(8,128)(2,1)}, u32[]{:S(2)}, u32[]{:S(2)}) collective-permute-start(bf16[384,1024]{1,0:T(8,128)(2,1)} %get-tuple-element.5), channel_id=1, source_target_pairs={{0,24},{8,0},{16,8},{24,16},{1,25},{9,1},{17,9},{25,17},{2,26},{10... | collective-permute-start | bytes 2359304 | tf_op jit(solution)/shard_map/ppermute | solution.py:34
  276.3 63.5 %collective-permute-start.1 = (bf16[384,1024]{1,0:T(8,128)(2,1)}, bf16[384,1024]{1,0:T(8,128)(2,1)}, u32[]{:S(2)}, u32[]{:S(2)}) collective-permute-start(bf16[384,1024]{1,0:T(8,128)(2,1)} %get-tuple-element.9), channel_id=1, source_target_pairs={{0,16},{8,24},{16,0},{24,8},{1,17},{9,25},{17,1},{25,9},{2,18},{10... | collective-permute-start | bytes 2359304 | tf_op jit(solution)/shard_map/ppermute | solution.py:34
  334.3 12.1 %collective-permute-start.2 = (bf16[384,1024]{1,0:T(8,128)(2,1)}, bf16[384,1024]{1,0:T(8,128)(2,1)}, u32[]{:S(2)}, u32[]{:S(2)}) collective-permute-start(bf16[384,1024]{1,0:T(8,128)(2,1)} %get-tuple-element.8), channel_id=1, source_target_pairs={{0,24},{8,0},{16,8},{24,16},{1,25},{9,1},{17,9},{25,17},{2,26},{10... | collective-permute-start | bytes 2359304 | tf_op jit(solution)/shard_map/ppermute | solution.py:34
  334.3 3.4 copy-start.8
  349.7 2.3 copy-start.2
  352.1 3.5 copy-start.3
  352.1 6.9 %copy-start.1 = (bf16[128,4096]{1,0:T(8,128)(2,1)S(1)}, bf16[128,4096]{1,0:T(8,128)(2,1)}, u32[]{:S(2)}) copy-start(bf16[128,4096]{1,0:T(8,128)(2,1)} %param.7) | copy-start | bytes 3145732
Sparse Core Ops, SparseCore 0:
  189.0 51.9 all-gather.2

commit v2 on v1

v2 whole, which is shorter than its diff:
```python
import functools

import jax
import jax.numpy as jnp
from jax import lax
from jax.experimental import pallas as pl
from jax.experimental.pallas import tpu as pltpu
from jax.sharding import PartitionSpec as P

F32 = jnp.float32
BF16 = jnp.bfloat16
CHUNKS = 4
CONTRACT = (((1,), (1,)), ((), ()))


def positions(half):
    me = lax.axis_index("expert")
    side = me // half
    local = me - side * half
    base = side * half
    partner = (1 - side) * half + local
    return me, side, local, base, partner


def meet(half, local, base, partner):
    barrier = pltpu.get_barrier_semaphore()
    for j in range(1, half):
        pl.semaphore_signal(barrier, inc=1, device_id={"expert": base + lax.rem(local + j, half)})
    pl.semaphore_signal(barrier, inc=1, device_id={"expert": partner})
    pl.semaphore_wait(barrier, half)


def remote(src, dst, send, recv, peer):
    return pltpu.make_async_remote_copy(
        src_ref=src, dst_ref=dst, send_sem=send, recv_sem=recv, device_id={"expert": peer}
    )


def dispatch_kernel(
    half, cap,
    sel, sel_t, tokens, out_grad, w_gate, w_up, w_down,
    arrived, incoming, hidden, gate_pre_grad, up_pre_grad, far_sel_t,
    far_sel, far_src, stage, pre_gate, pre_up, hidden_grad, vgate, vup, vdown,
    load_sem, sel_send, sel_recv, far_send, far_recv, near_send, near_recv,
):
    me, side, local, base, partner = positions(half)
    width = tokens.shape[1] // CHUNKS
    steps = 2 * CHUNKS
    loads = [
        pltpu.make_async_copy(a, b, load_sem.at[i])
        for i, (a, b) in enumerate(((w_gate, vgate), (w_up, vup), (w_down, vdown)))
    ]
    meet(half, local, base, partner)
    sources = (tokens, out_grad)
    landed = (arrived, incoming)
    sel_copies = [
        remote(sel.at[1 - side], far_sel, sel_send.at[0], sel_recv.at[0], partner),
        remote(sel_t.at[1 - side], far_sel_t, sel_send.at[1], sel_recv.at[1], partner),
    ]
    sel_copies[0].start()

    def columns(q):
        return pl.ds((q % CHUNKS) * width, width)

    far = [
        remote(sources[q // CHUNKS].at[:, columns(q)], far_src.at[q], far_send.at[q], far_recv.at[q], partner)
        for q in range(steps)
    ]
    started = [[] for _ in range(steps)]

    def rows_of(index):
        return pl.ds(pl.multiple_of(index * cap, 16), cap)

    def spread(q, kind, matrix, values, owner):
        part = q // CHUNKS
        slots = jnp.dot(matrix, values, preferred_element_type=F32).astype(BF16)
        stage[q, kind] = slots
        for j in range(1, half):
            peer = lax.rem(local + j, half)
            copy = remote(
                stage.at[q, kind, rows_of(peer)],
                landed[part].at[rows_of(owner), columns(q)],
                near_send.at[q, kind, j - 1],
                near_recv.at[q, kind, j - 1],
                base + peer,
            )
            copy.start()
            started[q].append(copy)
        landed[part][rows_of(owner), columns(q)] = stage[q, kind, rows_of(local)]

    far[0].start()
    for load in loads:
        load.start()
    for s in range(steps + 2):
        if s + 1 < steps:
            far[s + 1].start()
        if s == 0:
            sel_copies[1].start()
        if s < steps:
            part = s // CHUNKS
            spread(s, 0, sel[side, part], sources[part][:, columns(s)], me)
        if 1 <= s <= steps:
            q = s - 1
            if q == 0:
                sel_copies[0].wait_recv()
            far[q].wait_recv()
            spread(q, 1, far_sel[q // CHUNKS], far_src[q], partner)
        if s >= 2:
            q = s - 2
            for copy in started[q]:
                copy.wait_recv()
            part = q // CHUNKS
            rows = landed[part][:, columns(q)]
            if q == 0:
                loads[0].wait()
                loads[1].wait()
            if q == CHUNKS:
                loads[2].wait()
            if part == 0:
                for total, matrix in ((pre_gate, vgate), (pre_up, vup)):
                    term = jnp.dot(rows, matrix[columns(q), :], preferred_element_type=F32)
                    total[...] = term if q == 0 else total[...] + term
            else:
                term = lax.dot_general(rows, vdown[:, columns(q)], CONTRACT, preferred_element_type=F32)
                hidden_grad[...] = term if q == CHUNKS else hidden_grad[...] + term
    block = cap
    for start in range(0, pre_gate.shape[0], block):
        at = pl.ds(start, block)
        gate, up, grad = pre_gate[at, :], pre_up[at, :], hidden_grad[at, :]
        sigmoid = jax.nn.sigmoid(gate)
        silu = gate * sigmoid
        hidden[at, :] = (silu * up).astype(BF16)
        gate_pre_grad[at, :] = (grad * up * sigmoid * (1.0 + gate * (1.0 - sigmoid))).astype(BF16)
        up_pre_grad[at, :] = (grad * silu).astype(BF16)
    sel_copies[1].wait_recv()
    for copy in sel_copies + far:
        copy.wait_send()
    for q in range(steps):
        for copy in started[q]:
            copy.wait_send()


def return_kernel(
    half, cap,
    sel_t, far_sel_t, hidden, gate_pre_grad, up_pre_grad, w_gate, w_up, w_down,
    layer_out, tokens_grad,
    stage, back, part_send, part_recv, vgate, vup, vdown,
    load_sem, far_send, far_recv, near_send, near_recv,
):
    me, side, local, base, partner = positions(half)
    width = layer_out.shape[1] // CHUNKS
    steps = 2 * CHUNKS
    rows = half * cap
    loads = [
        pltpu.make_async_copy(a, b, load_sem.at[i])
        for i, (a, b) in enumerate(((w_down, vdown), (w_gate, vgate), (w_up, vup)))
    ]
    for load in loads:
        load.start()
    meet(half, local, base, partner)
    outs = (layer_out, tokens_grad)

    def columns(q):
        return pl.ds((q % CHUNKS) * width, width)

    def rows_of(index):
        return pl.ds(pl.multiple_of(index * cap, 16), cap)

    far = [
        remote(part_send_ref, part_recv_ref, far_send.at[q], far_recv.at[q], partner)
        for q, (part_send_ref, part_recv_ref) in enumerate(
            (part_send.at[q], part_recv.at[q]) for q in range(steps)
        )
    ]
    started = [([], []) for _ in range(steps)]
    for s in range(steps + 2):
        if s < steps:
            if s == 0:
                loads[0].wait()
            if s == CHUNKS:
                loads[1].wait()
                loads[2].wait()
            if s < CHUNKS:
                made = jnp.dot(hidden[...], vdown[:, columns(s)], preferred_element_type=F32)
            else:
                made = lax.dot_general(gate_pre_grad[...], vgate[columns(s), :], CONTRACT, preferred_element_type=F32)
                made = made + lax.dot_general(
                    up_pre_grad[...], vup[columns(s), :], CONTRACT, preferred_element_type=F32
                )
            stage[s] = made.astype(BF16)
            for kind in (1, 0):
                first = base if kind == 0 else half - base
                for j in range(1, half):
                    peer = lax.rem(local + j, half)
                    copy = remote(
                        stage.at[s, rows_of(first + peer)],
                        back.at[s, kind, rows_of(local)],
                        near_send.at[s, kind, j - 1],
                        near_recv.at[s, kind, j - 1],
                        base + peer,
                    )
                    copy.start()
                    started[s][kind].append(copy)
                back[s, kind, rows_of(local)] = stage[s, rows_of(first + local)]
        if 1 <= s <= steps:
            q = s - 1
            for copy in started[q][1]:
                copy.wait_recv()
            part_send[q] = jnp.dot(
                far_sel_t[1 - q // CHUNKS], back[q, 1], preferred_element_type=F32
            ).astype(BF16)
            far[q].start()
        if s >= 2:
            q = s - 2
            for copy in started[q][0]:
                copy.wait_recv()
            near = jnp.dot(sel_t[side, 1 - q // CHUNKS], back[q, 0], preferred_element_type=F32)
            far[q].wait_recv()
            outs[q // CHUNKS][:, columns(q)] = (near + part_recv[q].astype(F32)).astype(BF16)
    for q in range(steps):
        far[q].wait_send()
        for copies in started[q]:
            for copy in copies:
                copy.wait_send()


def selection(expert_ids, gate_codes, experts, capacity):
    tok_count = expert_ids.shape[0]
    expert_range = jnp.arange(experts, dtype=jnp.int32)
    named = expert_ids[:, :, None] == expert_range[None, None, :]
    chosen = jnp.any(named, axis=1).T
    gates = jnp.sum(jnp.where(named, gate_codes[:, :, None], 0), axis=1).T
    gates = gates.astype(jnp.float32) * (1.0 / 64.0)
    earlier = (
        jnp.arange(tok_count, dtype=jnp.int32)[:, None] < jnp.arange(tok_count, dtype=jnp.int32)[None, :]
    )
    ranks = jnp.dot(
        chosen.astype(jnp.bfloat16), earlier.astype(jnp.bfloat16), preferred_element_type=jnp.float32
    ).astype(jnp.int32)
    slots = jnp.where(chosen, ranks, -1)
    hit = slots[:, None, :] == jnp.arange(capacity, dtype=jnp.int32)[None, :, None]
    sel = hit.astype(jnp.bfloat16).reshape(experts * capacity, tok_count)
    sel_gate = jnp.where(hit, gates[:, None, :], 0.0).astype(jnp.bfloat16)
    return sel, sel_gate.reshape(experts * capacity, tok_count)


def swap_columns(rows, groups, me):
    width = rows.shape[1] // groups
    parts = [lax.dynamic_slice_in_dim(rows, me * width, width, axis=1)]
    for shift in range(1, groups):
        target = lax.rem(me + shift, groups)
        piece = lax.dynamic_slice_in_dim(rows, target * width, width, axis=1)
        parts.append(
            lax.ppermute(piece, "dp", [(i, (i + shift) % groups) for i in range(groups)])
        )
    return parts


def per_device(tokens, expert_ids, gate_codes, w_gate, w_up, w_down, out_grad):
    experts = lax.axis_size("expert")
    groups = lax.axis_size("dp")
    me = lax.axis_index("dp")
    tok_count, model_width = tokens.shape
    pair_count = tok_count * expert_ids.shape[1]
    capacity = 3 * pair_count // (2 * experts)
    half = experts // 2
    capacity = -(-capacity // 16) * 16
    rows = experts * capacity
    width = model_width // CHUNKS
    sel, sel_gate = selection(expert_ids, gate_codes, experts, capacity)
    both = jnp.stack([sel, sel_gate]).reshape(2, 2, half * capacity, tok_count)
    sides = both.transpose(1, 0, 2, 3)
    sides_t = both.transpose(1, 0, 3, 2)
    gate_matrix, up_matrix, down_matrix = w_gate[0], w_up[0], w_down[0]
    hidden_units = gate_matrix.shape[1]
    contract_rows = (((0,), (0,)), ((), ()))
    vmem = pl.BlockSpec(memory_space=pltpu.VMEM)
    anywhere = pl.BlockSpec(memory_space=pl.ANY)
    steps = 2 * CHUNKS
    dma = pltpu.SemaphoreType.DMA
    weights = [
        pltpu.VMEM((model_width, hidden_units), BF16),
        pltpu.VMEM((model_width, hidden_units), BF16),
        pltpu.VMEM((hidden_units, model_width), BF16),
    ]

    def shape(*dims):
        return jax.ShapeDtypeStruct(dims, BF16)

    arrived, incoming, hidden, gate_pre_grad, up_pre_grad, far_sel_t = pl.pallas_call(
        functools.partial(dispatch_kernel, half, capacity),
        out_shape=(
            shape(rows, model_width),
            shape(rows, model_width),
            shape(rows, hidden_units),
            shape(rows, hidden_units),
            shape(rows, hidden_units),
            shape(2, tok_count, half * capacity),
        ),
        in_specs=[vmem] * 4 + [anywhere] * 3,
        out_specs=(vmem,) * 6,
        scratch_shapes=[
            pltpu.VMEM((2, half * capacity, tok_count), BF16),
            pltpu.VMEM((steps, tok_count, width), BF16),
            pltpu.VMEM((steps, 2, half * capacity, width), BF16),
            pltpu.VMEM((rows, hidden_units), F32),
            pltpu.VMEM((rows, hidden_units), F32),
            pltpu.VMEM((rows, hidden_units), F32),
            *weights,
            dma((3,)),
            dma((2,)),
            dma((2,)),
            dma((steps,)),
            dma((steps,)),
            dma((steps, 2, half - 1)),
            dma((steps, 2, half - 1)),
        ],
        compiler_params=pltpu.CompilerParams(
            collective_id=0, has_side_effects=True, vmem_limit_bytes=56 * 2**20
        ),
    )(sides, sides_t, tokens, out_grad, gate_matrix, up_matrix, down_matrix)

    arrived_parts = swap_columns(arrived, groups, me)
    incoming_parts = swap_columns(incoming, groups, me)
    factors = jnp.concatenate([gate_pre_grad, up_pre_grad, hidden], axis=0)
    gathered = lax.all_gather(factors, "dp", axis=0, tiled=False)

    layer_out, tokens_grad = pl.pallas_call(
        functools.partial(return_kernel, half, capacity),
        out_shape=(shape(tok_count, model_width), shape(tok_count, model_width)),
        in_specs=[vmem] * 5 + [anywhere] * 3,
        out_specs=(vmem,) * 2,
        scratch_shapes=[
            pltpu.VMEM((steps, rows, width), BF16),
            pltpu.VMEM((steps, 2, half * capacity, width), BF16),
            pltpu.VMEM((steps, tok_count, width), BF16),
            pltpu.VMEM((steps, tok_count, width), BF16),
            *weights,
            dma((3,)),
            dma((steps,)),
            dma((steps,)),
            dma((steps, 2, half - 1)),
            dma((steps, 2, half - 1)),
        ],
        cost_estimate=pl.CostEstimate(
            flops=8 * rows * model_width * hidden_units, bytes_accessed=300_000_000, transcendentals=0
        ),
        compiler_params=pltpu.CompilerParams(
            collective_id=1, has_side_effects=True, vmem_limit_bytes=56 * 2**20
        ),
    )(sides_t, far_sel_t, hidden, gate_pre_grad, up_pre_grad, gate_matrix, up_matrix, down_matrix)

    gate_sum = up_sum = down_sum = 0.0
    for shift in range(groups):
        source = lax.rem(me - shift + groups, groups)
        factor = factors if shift == 0 else lax.dynamic_index_in_dim(gathered, source, 0, keepdims=False)
        tok, grad = arrived_parts[shift], incoming_parts[shift]
        gate_sum += lax.dot_general(tok, factor[:rows], contract_rows, preferred_element_type=F32)
        up_sum += lax.dot_general(
            tok, factor[rows : 2 * rows], contract_rows, preferred_element_type=F32
        )
        down_sum += lax.dot_general(
            factor[2 * rows :], grad, contract_rows, preferred_element_type=F32
        )
    return (
        layer_out.astype(BF16),
        tokens_grad.astype(BF16),
        gate_sum.astype(BF16)[None],
        up_sum.astype(BF16)[None],
        down_sum.astype(BF16)[None],
    )


def solution(mesh):
    placed = (
        P(("dp", "expert"), None),
        P(("dp", "expert"), None),
        P(("dp", "expert"), None),
        P("expert", None, None),
        P("expert", None, None),
        P("expert", None, None),
        P(("dp", "expert"), None),
    )
    return jax.shard_map(
        per_device,
        mesh=mesh,
        in_specs=placed,
        out_specs=(
            P(("dp", "expert"), None),
            P(("dp", "expert"), None),
            P("expert", "dp", None),
            P("expert", "dp", None),
            P("expert", None, "dp"),
        ),
        check_vma=False,
    )
```

time: 367 us -> 328 us (0.89)
  Pallas kernels: 0 us -> 262 us
  waiting for transfers between devices: 234 us -> 0.05 us
  matrix products: 82.9 us -> 32.7 us
  starting transfers between devices: 24.8 us -> 4.12 us
    pallas_call x0 -> x2, Pallas kernels: none -> 262 us  [the longest x1 134 us: per_device(): pl.pallas_call(functools.partial(dispatch_kernel, half, capacity), out_sh...]
    all_to_all x4 -> x0, waiting for transfers between devices: 234 us -> none  [exchange(): lax.all_to_all(rows, 'expert', split_axis=0, concat_axis=0, tiled=True)]
    dot_general x10 -> x0, matrix products: 51.3 us -> none  [the longest x1 8.74 us: per_device(): lax.dot_general(gate_pre_grad, gate_matrix, contract, preferred_element_t...]
    all_to_all x4 -> x0, starting transfers between devices: 20.8 us -> none  [exchange(): lax.all_to_all(rows, 'expert', split_axis=0, concat_axis=0, tiled=True)]
  transfers between devices with their start and end apart: 11 -> 7, of which waited for: 4 -> 0; matrix products, arithmetic and copies ran while one was open for 18% -> 10% of each run, Pallas kernels for 0% -> 39%
where the time goes in v2:
time: 328 us; the launch traced here: 327 us
  Pallas kernels  262 us (80%)
  matrix products  32.7 us (10%)
  between operations  14.3 us (4%)
  local copies, waits for them, and re-layouts  8.77 us (3%)
  other arithmetic  5 us (2%)
  starting transfers between devices  4.12 us (1%)
    pallas_call x1, Pallas kernels, per_device(): pl.pallas_call(functools.partial(dispatch_kernel, half, capacity), out_sh...  134 us
    pallas_call x1, Pallas kernels, per_device(): pl.pallas_call(functools.partial(return_kernel, half, capacity), out_shap...  128 us
    dot_general x4, matrix products, per_device(): lax.dot_general(factor[2 * rows:], grad, contract_rows, preferred_element...  11.8 us
    dot_general x4, matrix products, per_device(): lax.dot_general(tok, factor[rows:2 * rows], contract_rows, preferred_elem...  10.4 us
    dot_general x4, matrix products, per_device(): lax.dot_general(tok, factor[:rows], contract_rows, preferred_element_type...  10.3 us
  transfers between devices with their start and end apart: 7, of which 0 were waited for; matrix products, arithmetic and copies ran while one was open for 10% of the time, Pallas kernels for 39%

profile of v2, /device:TPU:0, one launch (start us, length us, event | category | flops | bytes accessed | tf_op | source)
XLA Modules:
  0.0 326.9 jit_solution(13374211590351304023)
XLA Ops:
  7.2 0.0 all-gather.3.cloned.1.call-start
  7.2 0.7 fusion.21
  7.9 0.1 fusion.3
  8.1 0.1 copy.21
  8.2 0.1 eq.51
  8.3 0.7 select_reduce_fusion
  9.0 0.1 copy.22
  9.1 0.1 fusion.34
  9.2 0.7 fusion.19
  10.0 0.8 copy.23.sel
  10.8 134.1 %shard_map.110 = (bf16[384,4096]{1,0:T(8,128)(2,1)}, bf16[384,4096]{1,0:T(8,128)(2,1)}, bf16[384,768]{1,0:T(8,128)(2,1)}, bf16[384,768]{1,0:T(8,128)(2,1)}, bf16...) custom-call(bf16[2,2,192,128]{3,2,1,0:T(8,128)(2,1)} %copy.23.sel, bf16[2,2,128,192]{3,2,1,0:T(8,128)(2,1)} %get-tuple-element.30.sel_t, ...), custom_call_target="tpu_custom_call" | custom-call | tf_op jit(solution)/shard_map/pallas_call | solution.py:290
  144.9 2.8 pad_maximum_fusion
  147.7 0.0 copy-start.2
  147.7 0.0 all-gather.3.cloned.1.call-update
  147.7 3.2 constant_dynamic-slice_fusion
  151.0 1.5 collective-permute-start.4
  152.5 0.0 collective-permute-start.3
  152.5 1.8 collective-permute-start.5
  154.3 0.0 copy-done.2
  154.3 1.5 constant_dynamic-slice_fusion.3
  155.7 0.0 collective-permute-start
  155.7 0.5 collective-permute-start.1
  156.2 0.0 copy-start.3
  156.2 127.9 %shard_map.111 = (bf16[128,4096]{1,0:T(8,128)(2,1)}, bf16[128,4096]{1,0:T(8,128)(2,1)}) custom-call(bf16[2,2,128,192]{3,2,1,0:T(8,128)(2,1)} %get-tuple-element.30.sel_t, bf16[2,128,192]{2,1,0:T(8,128)(2,1)} %get-tuple-element.13.far_sel_t, bf16[384,768]{1,0:T(8,128)(2,1)} %get-tuple-element.14.hidden, bf16[384,768]{1,0:T(8,128)(2,1)} %get-tuple-element.15.gate_pre_grad, ...), custom_call_target="tpu_custom_call" | custom-call | flops 9663676416 | bytes 300000000 | tf_op jit(solution)/shard_map/pallas_call | solution.py:328
  284.1 0.0 copy-done.3
  284.1 0.0 copy-start.6
  284.1 3.8 %fusion.4 = f32[768,1024]{1,0:T(8,128)} fusion(bf16[384,768]{1,0:T(8,128)(2,1)S(1)} %copy-done.3, bf16[384,4096]{1,0:T(8,128)(2,1)} %get-tuple-element.20, s32[]{:T(128)S(6)} %select_n.49), kind=kOutput, calls=%fused_computation.9 | convolution fusion | flops 603979776 | bytes 4521988 | tf_op jit(solution)/shard_map/dot_general | solution.py:362
  288.0 0.0 copy-done.6
  288.0 0.0 copy-start.5
  288.0 2.8 fusion.6
  290.7 0.0 copy-done.5
  290.7 2.1 fusion.8
  292.9 0.0 collective-permute-done
  292.9 0.3 collective-permute-start.2
  293.2 0.0 all-gather.3.cloned.1.call-done
  293.2 0.0 copy-start.4
  293.2 2.5 fusion.18
  295.7 0.9 copy-done.4
  296.7 2.1 fusion.15
  298.8 0.0 collective-permute-done.1
  298.8 2.2 fusion.14
  301.0 2.2 fusion.17
  303.1 0.0 copy-start
  303.2 0.0 collective-permute-done.4
  303.2 2.3 fusion.11
  305.5 0.0 collective-permute-done.2
  305.5 0.0 copy-done
  305.5 3.4 %fusion.1 = bf16[1,1024,768]{2,1,0:T(8,128)(2,1)} fusion(f32[1024,768]{1,0:T(8,128)S(1)} %fusion.14, f32[1024,768]{1,0:T(8,128)S(1)} %copy-done, f32[1024,768]{1,0:T(8,128)S(1)} %fusion.15, bf16[384,1024]{1,0:T(8,128)(2,1)} %collective-permute-done.2, bf16[4,1152,768]{2,1,0:T(8,128)(2,1)S(1)} %bitcast.77, s32[]{:T(128)S(6)} %select_n.55, s32[]{:T(128)S(6)} %add.96), kind=kOutput, calls=%fused_computation.5 | convolution fusion | flops 607125504 | bytes 12386312 | tf_op jit(solution)/shard_map/dot_general | solution.py:359
  308.9 0.0 collective-permute-done.3
  308.9 2.1 fusion.12
  311.0 0.0 copy-start.1
  311.0 3.5 %fusion = bf16[1,1024,768]{2,1,0:T(8,128)(2,1)} fusion(f32[1024,768]{1,0:T(8,128)S(1)} %fusion.17, f32[1024,768]{1,0:T(8,128)S(1)} %fusion.8, f32[1024,768]{1,0:T(8,128)S(1)} %fusion.18, bf16[384,1024]{1,0:T(8,128)(2,1)} %collective-permute-done.2, bf16[4,1152,768]{2,1,0:T(8,128)(2,1)S(1)} %bitcast.79, s32[]{:T(128)S(6)} %select_n.55), kind=kOutput, calls=%fused_computation.4 | convolution fusion | flops 607125504 | bytes 12386308 | tf_op jit(solution)/shard_map/dot_general | solution.py:358
  314.5 0.0 copy-start.8
  314.5 0.0 copy-start.7
  314.5 0.0 collective-permute-done.5
  314.5 0.0 copy-done.1
  314.5 3.6 %fusion.2 = bf16[1,768,1024]{2,1,0:T(8,128)(2,1)} fusion(f32[768,1024]{1,0:T(8,128)S(1)} %fusion.11, f32[768,1024]{1,0:T(8,128)S(1)} %copy-done.1, f32[768,1024]{1,0:T(8,128)S(1)} %fusion.12, bf16[384,1024]{1,0:T(8,128)(2,1)} %collective-permute-done.5, bf16[4,1152,768]{2,1,0:T(8,128)(2,1)S(1)} %bitcast.80, s32[]{:T(128)S(6)} %select_n.55, s32[]{:T(128)S(6)} %add.99), kind=kOutput, calls=%fused_computation.6 | convolution fusion | flops 607125504 | bytes 12386312 | tf_op jit(solution)/shard_map/dot_general | solution.py:362
  318.1 0.0 copy-done.8
  318.1 1.0 copy.26
  319.1 0.0 copy-done.7
  319.1 1.0 copy.27
  (5 shorter events, 0.1 us)
Async XLA Ops:
  7.2 286.1 %all-gather.3.cloned.1.call-start = ((), (), s32[]{:S(2)}) async-start(), calls=%async_computation | async-start | bytes 8847360 | tf_op jit(solution)/shard_map/all_gather | solution.py:326
  147.7 6.6 %copy-start.2 = (bf16[384,4096]{1,0:T(8,128)(2,1)S(1)}, bf16[384,4096]{1,0:T(8,128)(2,1)}, u32[]{:S(2)}) copy-start(bf16[384,4096]{1,0:T(8,128)(2,1)} %get-tuple-element.19) | copy-start | bytes 9437188
  151.0 152.2 %collective-permute-start.4 = (bf16[384,1024]{1,0:T(8,128)(2,1)}, bf16[384,1024]{1,0:T(8,128)(2,1)}, u32[]{:S(2)}, u32[]{:S(2)}) collective-permute-start(bf16[384,1024]{1,0:T(8,128)(2,1)} %get-tuple-element.24), channel_id=1, source_target_pairs={{0,16},{8,24},{16,0},{24,8},{1,17},{9,25},{17,1},{25,9},{2,18},{10... | collective-permute-start | bytes 2359304 | tf_op jit(solution)/shard_map/ppermute | solution.py:254
  152.5 156.4 %collective-permute-start.3 = (bf16[384,1024]{1,0:T(8,128)(2,1)}, bf16[384,1024]{1,0:T(8,128)(2,1)}, u32[]{:S(2)}, u32[]{:S(2)}) collective-permute-start(bf16[384,1024]{1,0:T(8,128)(2,1)} %get-tuple-element.25), channel_id=1, source_target_pairs={{0,8},{8,16},{16,24},{24,0},{1,9},{9,17},{17,25},{25,1},{2,10},{10... | collective-permute-start | bytes 2359304 | tf_op jit(solution)/shard_map/ppermute | solution.py:254
  152.5 162.0 %collective-permute-start.5 = (bf16[384,1024]{1,0:T(8,128)(2,1)}, bf16[384,1024]{1,0:T(8,128)(2,1)}, u32[]{:S(2)}, u32[]{:S(2)}) collective-permute-start(bf16[384,1024]{1,0:T(8,128)(2,1)} %get-tuple-element.23), channel_id=1, source_target_pairs={{0,24},{8,0},{16,8},{24,16},{1,25},{9,1},{17,9},{25,17},{2,26},{10... | collective-permute-start | bytes 2359304 | tf_op jit(solution)/shard_map/ppermute | solution.py:254
  155.7 137.2 %collective-permute-start = (bf16[384,1024]{1,0:T(8,128)(2,1)}, bf16[384,1024]{1,0:T(8,128)(2,1)}, u32[]{:S(2)}, u32[]{:S(2)}) collective-permute-start(bf16[384,1024]{1,0:T(8,128)(2,1)} %get-tuple-element.28), channel_id=1, source_target_pairs={{0,8},{8,16},{16,24},{24,0},{1,9},{9,17},{17,25},{25,1},{2,10},{10... | collective-permute-start | bytes 2359304 | tf_op jit(solution)/shard_map/ppermute | solution.py:254
  155.7 143.1 %collective-permute-start.1 = (bf16[384,1024]{1,0:T(8,128)(2,1)}, bf16[384,1024]{1,0:T(8,128)(2,1)}, u32[]{:S(2)}, u32[]{:S(2)}) collective-permute-start(bf16[384,1024]{1,0:T(8,128)(2,1)} %get-tuple-element.27), channel_id=1, source_target_pairs={{0,16},{8,24},{16,0},{24,8},{1,17},{9,25},{17,1},{25,9},{2,18},{10... | collective-permute-start | bytes 2359304 | tf_op jit(solution)/shard_map/ppermute | solution.py:254
  156.2 127.9 %copy-start.3 = (bf16[384,768]{1,0:T(8,128)(2,1)S(1)}, bf16[384,768]{1,0:T(8,128)(2,1)}, u32[]{:S(2)}) copy-start(bf16[384,768]{1,0:T(8,128)(2,1)} %get-tuple-element.14.hidden) | copy-start | bytes 1769476
  284.1 3.9 %copy-start.6 = (bf16[384,768]{1,0:T(8,128)(2,1)S(1)}, bf16[384,768]{1,0:T(8,128)(2,1)}, u32[]{:S(2)}) copy-start(bf16[384,768]{1,0:T(8,128)(2,1)} %get-tuple-element.16.up_pre_grad) | copy-start | bytes 1769476
  288.0 2.8 copy-start.5
  292.9 12.6 %collective-permute-start.2 = (bf16[384,1024]{1,0:T(8,128)(2,1)}, bf16[384,1024]{1,0:T(8,128)(2,1)}, u32[]{:S(2)}, u32[]{:S(2)}) collective-permute-start(bf16[384,1024]{1,0:T(8,128)(2,1)} %get-tuple-element.26), channel_id=1, source_target_pairs={{0,24},{8,0},{16,8},{24,16},{1,25},{9,1},{17,9},{25,17},{2,26},{10... | collective-permute-start | bytes 2359304 | tf_op jit(solution)/shard_map/ppermute | solution.py:254
  293.2 3.4 %copy-start.4 = (bf16[4608,768]{1,0:T(8,128)(2,1)S(1)}, bf16[4608,768]{1,0:T(8,128)(2,1)}, u32[]{:S(2)}) copy-start(bf16[4608,768]{1,0:T(8,128)(2,1)} %all-gather.3.cloned.1.call-done) | copy-start | bytes 21233668
  303.1 2.3 copy-start
  311.0 3.5 %copy-start.1 = (f32[768,1024]{1,0:T(8,128)S(1)}, f32[768,1024]{1,0:T(8,128)}, u32[]{:S(2)}) copy-start(f32[768,1024]{1,0:T(8,128)} %fusion.4) | copy-start | bytes 9437188
  314.5 3.6 %copy-start.8 = (bf16[128,4096]{1,0:T(8,128)(2,1)S(1)}, bf16[128,4096]{1,0:T(8,128)(2,1)}, u32[]{:S(2)}) copy-start(bf16[128,4096]{1,0:T(8,128)(2,1)} %get-tuple-element.36) | copy-start | bytes 3145732
  314.5 4.5 %copy-start.7 = (bf16[128,4096]{1,0:T(8,128)(2,1)S(1)}, bf16[128,4096]{1,0:T(8,128)(2,1)}, u32[]{:S(2)}) copy-start(bf16[128,4096]{1,0:T(8,128)(2,1)} %get-tuple-element.37) | copy-start | bytes 3145732
Sparse Core Ops, SparseCore 0:
  147.8 88.7 all-gather.2

commit v3 on v2

v3 whole, which is shorter than its diff:
```python
import functools

import jax
import jax.numpy as jnp
from jax import lax
from jax.experimental import pallas as pl
from jax.experimental.pallas import tpu as pltpu
from jax.sharding import PartitionSpec as P

F32 = jnp.float32
BF16 = jnp.bfloat16
CONTRACT = (((1,), (1,)), ((), ()))


def positions(half):
    me = lax.axis_index("expert")
    side = me // half
    local = me - side * half
    base = side * half
    partner = (1 - side) * half + local
    return me, side, local, base, partner


def meet(half, local, base, partner, groups, group):
    barrier = pltpu.get_barrier_semaphore()
    for shift in range(1, groups):
        pl.semaphore_signal(barrier, inc=1, device_id={"dp": lax.rem(group + shift, groups)})
    for j in range(1, half):
        pl.semaphore_signal(barrier, inc=1, device_id={"expert": base + lax.rem(local + j, half)})
    pl.semaphore_signal(barrier, inc=1, device_id={"expert": partner})
    pl.semaphore_wait(barrier, half + groups - 1)


def remote(src, dst, send, recv, peer, axis="expert"):
    return pltpu.make_async_remote_copy(
        src_ref=src, dst_ref=dst, send_sem=send, recv_sem=recv, device_id={axis: peer}
    )


def dispatch_kernel(
    half, cap, groups, chunks,
    sel, sel_t, tokens, out_grad, w_gate, w_up, w_down,
    token_cols, grad_cols, all_hidden, hidden, gate_pre_grad, up_pre_grad, far_sel_t,
    arrived, incoming, far_sel, far_src, stage, pre_gate, pre_up, hidden_grad, vgate, vup, vdown,
    load_sem, sel_send, sel_recv, far_send, far_recv, near_send, near_recv, group_send, group_recv,
):
    me, side, local, base, partner = positions(half)
    group = lax.axis_index("dp")
    width = tokens.shape[1] // chunks
    block = tokens.shape[1] // groups
    per_block = chunks // groups
    steps = 2 * chunks
    loads = [
        pltpu.make_async_copy(a, b, load_sem.at[i])
        for i, (a, b) in enumerate(((w_gate, vgate), (w_up, vup), (w_down, vdown)))
    ]
    meet(half, local, base, partner, groups, group)
    sources = (tokens, out_grad)
    landed = (arrived, incoming)
    sel_copies = [
        remote(sel.at[1 - side], far_sel, sel_send.at[0], sel_recv.at[0], partner),
        remote(sel_t.at[1 - side], far_sel_t, sel_send.at[1], sel_recv.at[1], partner),
    ]
    sel_copies[0].start()

    def block_columns(shift):
        return pl.ds(pl.multiple_of(lax.rem(group + shift, groups) * block, 128), block)

    def columns(q):
        shift, inner = divmod(q % chunks, per_block)
        start = lax.rem(group + shift, groups) * block + inner * width
        return pl.ds(pl.multiple_of(start, 128), width)

    group_copies = []

    def to_group(source, target, shift, kind):
        if shift == 0:
            copy = pltpu.make_async_copy(source, target.at[0], group_send.at[kind, 0])
        else:
            copy = remote(
                source, target.at[shift], group_send.at[kind, shift], group_recv.at[kind, shift],
                lax.rem(group + shift, groups), "dp",
            )
        copy.start()
        group_copies.append((shift, copy))

    far = [
        remote(sources[q // chunks].at[:, columns(q)], far_src.at[q], far_send.at[q], far_recv.at[q], partner)
        for q in range(steps)
    ]
    started = [[] for _ in range(steps)]

    def rows_of(index):
        return pl.ds(pl.multiple_of(index * cap, 16), cap)

    def spread(q, kind, matrix, values, owner):
        part = q // chunks
        slots = jnp.dot(matrix, values, preferred_element_type=F32).astype(BF16)
        stage[q, kind] = slots
        for j in range(1, half):
            peer = lax.rem(local + j, half)
            copy = remote(
                stage.at[q, kind, rows_of(peer)],
                landed[part].at[rows_of(owner), columns(q)],
                near_send.at[q, kind, j - 1],
                near_recv.at[q, kind, j - 1],
                base + peer,
            )
            copy.start()
            started[q].append(copy)
        landed[part][rows_of(owner), columns(q)] = stage[q, kind, rows_of(local)]

    far[0].start()
    for load in loads:
        load.start()
    for s in range(steps + 2):
        if s + 1 < steps:
            far[s + 1].start()
        if s == 0:
            sel_copies[1].start()
        if s < steps:
            part = s // chunks
            spread(s, 0, sel[side, part], sources[part][:, columns(s)], me)
        if 1 <= s <= steps:
            q = s - 1
            if q == 0:
                sel_copies[0].wait_recv()
            far[q].wait_recv()
            spread(q, 1, far_sel[q // chunks], far_src[q], partner)
        if s >= 2:
            q = s - 2
            for copy in started[q]:
                copy.wait_recv()
            part = q // chunks
            rows = landed[part][:, columns(q)]
            if q == 0:
                loads[0].wait()
                loads[1].wait()
            if q == chunks:
                loads[2].wait()
            if (q + 1) % per_block == 0:
                shift = (q % chunks) // per_block
                to_group(landed[part].at[:, block_columns(shift)], (token_cols, grad_cols)[part], shift, part)
            if part == 0:
                for total, matrix in ((pre_gate, vgate), (pre_up, vup)):
                    term = jnp.dot(rows, matrix[columns(q), :], preferred_element_type=F32)
                    total[...] = term if q == 0 else total[...] + term
                if q == chunks - 1:
                    for start in range(0, pre_gate.shape[0], cap):
                        at = pl.ds(start, cap)
                        gate = pre_gate[at, :]
                        hidden[at, :] = (gate * jax.nn.sigmoid(gate) * pre_up[at, :]).astype(BF16)
                    for shift in range(groups):
                        to_group(hidden, all_hidden, shift, 2)
            else:
                term = lax.dot_general(rows, vdown[:, columns(q)], CONTRACT, preferred_element_type=F32)
                hidden_grad[...] = term if q == chunks else hidden_grad[...] + term
    for start in range(0, pre_gate.shape[0], cap):
        at = pl.ds(start, cap)
        gate, up, grad = pre_gate[at, :], pre_up[at, :], hidden_grad[at, :]
        sigmoid = jax.nn.sigmoid(gate)
        silu = gate * sigmoid
        gate_pre_grad[at, :] = (grad * up * sigmoid * (1.0 + gate * (1.0 - sigmoid))).astype(BF16)
        up_pre_grad[at, :] = (grad * silu).astype(BF16)
    for shift, copy in group_copies:
        if shift == 0:
            copy.wait()
        else:
            copy.wait_recv()
            copy.wait_send()
    sel_copies[1].wait_recv()
    for copy in sel_copies + far:
        copy.wait_send()
    for q in range(steps):
        for copy in started[q]:
            copy.wait_send()


def return_kernel(
    half, cap, groups, chunks,
    sel_t, far_sel_t, hidden, gate_pre_grad, up_pre_grad, token_cols, grad_cols, all_hidden,
    w_gate, w_up, w_down,
    layer_out, tokens_grad, gate_sum, up_sum, down_sum, factors,
    stage, back, part_send, part_recv, vgate, vup, vdown, left, right, gate_total, up_total, down_total,
    load_sem, far_send, far_recv, near_send, near_recv, group_send, group_recv, piece_sem,
):
    me, side, local, base, partner = positions(half)
    group = lax.axis_index("dp")
    width = layer_out.shape[1] // chunks
    steps = 2 * chunks
    own = (gate_pre_grad, up_pre_grad)
    rows = half * cap
    loads = [
        pltpu.make_async_copy(a, b, load_sem.at[i])
        for i, (a, b) in enumerate(((w_down, vdown), (w_gate, vgate), (w_up, vup)))
    ]
    for load in loads:
        load.start()
    meet(half, local, base, partner, groups, group)
    group_copies = {}
    for shift in range(1, groups):
        for kind in (0, 1):
            copy = remote(
                own[kind], factors.at[shift, kind], group_send.at[shift, kind], group_recv.at[shift, kind],
                lax.rem(group + shift, groups), "dp",
            )
            copy.start()
            group_copies[shift, kind] = copy

    def piece_loads(i):
        slot, source = i % 2, i % groups
        if i < groups:
            pairs = [(grad_cols.at[source], left.at[slot]), (all_hidden.at[source], right.at[slot, 0])]
        else:
            pairs = [(token_cols.at[source], left.at[slot])]
            for kind in (0, 1):
                held = own[kind] if source == 0 else factors.at[source, kind]
                pairs.append((held, right.at[slot, kind]))
        return [pltpu.make_async_copy(a, b, piece_sem.at[i, n]) for n, (a, b) in enumerate(pairs)]

    def start_piece(i):
        if i > groups:
            for kind in (0, 1):
                group_copies[i % groups, kind].wait_recv()
        copies = piece_loads(i)
        for copy in copies:
            copy.start()
        return copies

    def accumulate(total, result, at, term, i):
        source = i % groups
        if source > 0:
            term = total[at, :] + term
        if source < groups - 1:
            total[at, :] = term
        else:
            result[at, :] = term.astype(BF16)

    def run_piece(i, copies):
        for copy in copies:
            copy.wait()
        slot = i % 2
        rows_first = (((0,), (0,)), ((), ()))
        if i < groups:
            for start in range(0, down_sum.shape[0], 256):
                at = pl.ds(start, 256)
                term = lax.dot_general(right[slot, 0, :, at], left[slot], rows_first, preferred_element_type=F32)
                accumulate(down_total, down_sum, at, term, i)
        else:
            for start in range(0, gate_sum.shape[0], 256):
                at = pl.ds(start, 256)
                for kind, total, result in ((0, gate_total, gate_sum), (1, up_total, up_sum)):
                    term = lax.dot_general(left[slot, :, at], right[slot, kind], rows_first, preferred_element_type=F32)
                    accumulate(total, result, at, term, i)

    when = {1 + g: g for g in range(groups)}
    when.update({chunks + 2 + g: groups + g for g in range(groups)})
    pending = {0: start_piece(0)}
    outs = (layer_out, tokens_grad)

    def columns(q):
        return pl.ds((q % chunks) * width, width)

    def rows_of(index):
        return pl.ds(pl.multiple_of(index * cap, 16), cap)

    far = [
        remote(part_send_ref, part_recv_ref, far_send.at[q], far_recv.at[q], partner)
        for q, (part_send_ref, part_recv_ref) in enumerate(
            (part_send.at[q], part_recv.at[q]) for q in range(steps)
        )
    ]
    started = [([], []) for _ in range(steps)]
    for s in range(steps + 2):
        if s < steps:
            if s == 0:
                loads[0].wait()
            if s == chunks:
                loads[1].wait()
                loads[2].wait()
            if s < chunks:
                made = jnp.dot(hidden[...], vdown[:, columns(s)], preferred_element_type=F32)
            else:
                made = lax.dot_general(gate_pre_grad[...], vgate[columns(s), :], CONTRACT, preferred_element_type=F32)
                made = made + lax.dot_general(
                    up_pre_grad[...], vup[columns(s), :], CONTRACT, preferred_element_type=F32
                )
            slot = s % chunks
            if s >= chunks:
                for copies in started[s - chunks]:
                    for copy in copies:
                        copy.wait_send()
            stage[slot] = made.astype(BF16)
            for kind in (1, 0):
                first = base if kind == 0 else half - base
                for j in range(1, half):
                    peer = lax.rem(local + j, half)
                    copy = remote(
                        stage.at[slot, rows_of(first + peer)],
                        back.at[s, kind, rows_of(local)],
                        near_send.at[s, kind, j - 1],
                        near_recv.at[s, kind, j - 1],
                        base + peer,
                    )
                    copy.start()
                    started[s][kind].append(copy)
                back[s, kind, rows_of(local)] = stage[slot, rows_of(first + local)]
        if 1 <= s <= steps:
            q = s - 1
            for copy in started[q][1]:
                copy.wait_recv()
            part_send[q] = jnp.dot(
                far_sel_t[1 - q // chunks], back[q, 1], preferred_element_type=F32
            ).astype(BF16)
            far[q].start()
        if s in when:
            i = when[s]
            if i + 1 < 2 * groups and i + 1 != groups + 1:
                pending[i + 1] = start_piece(i + 1)
            if i not in pending:
                pending[i] = start_piece(i)
            run_piece(i, pending[i])
        if s >= 2:
            q = s - 2
            for copy in started[q][0]:
                copy.wait_recv()
            near = jnp.dot(sel_t[side, 1 - q // chunks], back[q, 0], preferred_element_type=F32)
            far[q].wait_recv()
            outs[q // chunks][:, columns(q)] = (near + part_recv[q].astype(F32)).astype(BF16)
    for copy in far:
        copy.wait_send()
    for q in range(chunks, steps):
        for copies in started[q]:
            for copy in copies:
                copy.wait_send()
    for copy in group_copies.values():
        copy.wait_send()


def selection(expert_ids, gate_codes, experts, capacity):
    tok_count = expert_ids.shape[0]
    expert_range = jnp.arange(experts, dtype=jnp.int32)
    named = expert_ids[:, :, None] == expert_range[None, None, :]
    chosen = jnp.any(named, axis=1).T
    gates = jnp.sum(jnp.where(named, gate_codes[:, :, None], 0), axis=1).T
    gates = gates.astype(jnp.float32) * (1.0 / 64.0)
    earlier = (
        jnp.arange(tok_count, dtype=jnp.int32)[:, None] < jnp.arange(tok_count, dtype=jnp.int32)[None, :]
    )
    ranks = jnp.dot(
        chosen.astype(jnp.bfloat16), earlier.astype(jnp.bfloat16), preferred_element_type=jnp.float32
    ).astype(jnp.int32)
    slots = jnp.where(chosen, ranks, -1)
    hit = slots[:, None, :] == jnp.arange(capacity, dtype=jnp.int32)[None, :, None]
    sel = hit.astype(jnp.bfloat16).reshape(experts * capacity, tok_count)
    sel_gate = jnp.where(hit, gates[:, None, :], 0.0).astype(jnp.bfloat16)
    return sel, sel_gate.reshape(experts * capacity, tok_count)


def per_device(tokens, expert_ids, gate_codes, w_gate, w_up, w_down, out_grad):
    experts = lax.axis_size("expert")
    groups = lax.axis_size("dp")
    tok_count, model_width = tokens.shape
    pair_count = tok_count * expert_ids.shape[1]
    capacity = 3 * pair_count // (2 * experts)
    half = experts // 2
    capacity = -(-capacity // 16) * 16
    rows = experts * capacity
    chunks = groups * max(1, 8 // groups)
    width = model_width // chunks
    block = model_width // groups
    sel, sel_gate = selection(expert_ids, gate_codes, experts, capacity)
    both = jnp.stack([sel, sel_gate]).reshape(2, 2, half * capacity, tok_count)
    sides = both.transpose(1, 0, 2, 3)
    sides_t = both.transpose(1, 0, 3, 2)
    gate_matrix, up_matrix, down_matrix = w_gate[0], w_up[0], w_down[0]
    hidden_units = gate_matrix.shape[1]
    vmem = pl.BlockSpec(memory_space=pltpu.VMEM)
    anywhere = pl.BlockSpec(memory_space=pl.ANY)
    steps = 2 * chunks
    dma = pltpu.SemaphoreType.DMA
    weights = [
        pltpu.VMEM((model_width, hidden_units), BF16),
        pltpu.VMEM((model_width, hidden_units), BF16),
        pltpu.VMEM((hidden_units, model_width), BF16),
    ]

    def shape(*dims):
        return jax.ShapeDtypeStruct(dims, BF16)

    token_cols, grad_cols, all_hidden, hidden, gate_pre_grad, up_pre_grad, far_sel_t = pl.pallas_call(
        functools.partial(dispatch_kernel, half, capacity, groups, chunks),
        out_shape=(
            shape(groups, rows, block),
            shape(groups, rows, block),
            shape(groups, rows, hidden_units),
            shape(rows, hidden_units),
            shape(rows, hidden_units),
            shape(rows, hidden_units),
            shape(2, tok_count, half * capacity),
        ),
        in_specs=[vmem] * 4 + [anywhere] * 3,
        out_specs=(anywhere,) * 3 + (vmem,) * 4,
        scratch_shapes=[
            pltpu.VMEM((rows, model_width), BF16),
            pltpu.VMEM((rows, model_width), BF16),
            pltpu.VMEM((2, half * capacity, tok_count), BF16),
            pltpu.VMEM((steps, tok_count, width), BF16),
            pltpu.VMEM((steps, 2, half * capacity, width), BF16),
            pltpu.VMEM((rows, hidden_units), F32),
            pltpu.VMEM((rows, hidden_units), F32),
            pltpu.VMEM((rows, hidden_units), F32),
            *weights,
            dma((3,)),
            dma((2,)),
            dma((2,)),
            dma((steps,)),
            dma((steps,)),
            dma((steps, 2, half - 1)),
            dma((steps, 2, half - 1)),
            dma((3, groups)),
            dma((3, groups)),
        ],
        compiler_params=pltpu.CompilerParams(
            collective_id=0, has_side_effects=True, vmem_limit_bytes=56 * 2**20
        ),
    )(sides, sides_t, tokens, out_grad, gate_matrix, up_matrix, down_matrix)

    layer_out, tokens_grad, gate_sum, up_sum, down_sum, _ = pl.pallas_call(
        functools.partial(return_kernel, half, capacity, groups, chunks),
        out_shape=(
            shape(tok_count, model_width),
            shape(tok_count, model_width),
            shape(block, hidden_units),
            shape(block, hidden_units),
            shape(hidden_units, block),
            shape(groups, 2, rows, hidden_units),
        ),
        in_specs=[vmem] * 5 + [anywhere] * 6,
        out_specs=(vmem,) * 5 + (anywhere,),
        scratch_shapes=[
            pltpu.VMEM((chunks, rows, width), BF16),
            pltpu.VMEM((steps, 2, half * capacity, width), BF16),
            pltpu.VMEM((steps, tok_count, width), BF16),
            pltpu.VMEM((steps, tok_count, width), BF16),
            *weights,
            pltpu.VMEM((2, rows, block), BF16),
            pltpu.VMEM((2, 2, rows, hidden_units), BF16),
            pltpu.VMEM((block, hidden_units), F32),
            pltpu.VMEM((block, hidden_units), F32),
            pltpu.VMEM((hidden_units, block), F32),
            dma((3,)),
            dma((steps,)),
            dma((steps,)),
            dma((steps, 2, half - 1)),
            dma((steps, 2, half - 1)),
            dma((groups, 2)),
            dma((groups, 2)),
            dma((2 * groups, 3)),
        ],
        compiler_params=pltpu.CompilerParams(
            collective_id=1, has_side_effects=True, vmem_limit_bytes=63 * 2**20
        ),
    )(
        sides_t, far_sel_t, hidden, gate_pre_grad, up_pre_grad, token_cols, grad_cols, all_hidden,
        gate_matrix, up_matrix, down_matrix,
    )
    return layer_out, tokens_grad, gate_sum[None], up_sum[None], down_sum[None]


def solution(mesh):
    placed = (
        P(("dp", "expert"), None),
        P(("dp", "expert"), None),
        P(("dp", "expert"), None),
        P("expert", None, None),
        P("expert", None, None),
        P("expert", None, None),
        P(("dp", "expert"), None),
    )
    return jax.shard_map(
        per_device,
        mesh=mesh,
        in_specs=placed,
        out_specs=(
            P(("dp", "expert"), None),
            P(("dp", "expert"), None),
            P("expert", "dp", None),
            P("expert", "dp", None),
            P("expert", None, "dp"),
        ),
        check_vma=False,
    )
```

time: 328 us -> 300 us (0.915)
  matrix products: 32.7 us -> 0.14 us
  Pallas kernels: 262 us -> 287 us
  between operations: 14.3 us -> 0.71 us
  starting transfers between devices: 4.12 us -> 0 us
    dot_general x12 -> x0, matrix products: 32.5 us -> none  [the longest x4 11.8 us: per_device(): lax.dot_general(factor[2 * rows:], grad, contract_rows, preferred_element...]
    pallas_call x2, Pallas kernels: 262 us -> 287 us  [the longest x1 156 us: per_device(): pl.pallas_call(functools.partial(dispatch_kernel, half, capacity, groups,...]
    unnamed x20 -> x11, local copies, waits for them, and re-layouts: 2.91 us -> 9.08 us
    dynamic_slice x2 -> x0, local copies, waits for them, and re-layouts: 4.69 us -> none  [swap_columns(): piece = lax.dynamic_slice_in_dim(rows, target * width, width, axis=1)]
    ppermute x6 -> x0, starting transfers between devices: 4.08 us -> none  [swap_columns(): lax.ppermute(piece, 'dp', [(i, (i + shift) % groups) for i in range(group...]
  transfers between devices with their start and end apart: 7 -> 0, of which waited for: 0 -> 0; matrix products, arithmetic and copies ran while one was open for 10% -> 0% of each run, Pallas kernels for 39% -> 0%
where the time goes in v3:
time: 300 us
  Pallas kernels  287 us (96%)
  local copies, waits for them, and re-layouts  10.2 us (3%)
    pallas_call x1, Pallas kernels, per_device(): pl.pallas_call(functools.partial(dispatch_kernel, half, capacity, groups,...  156 us
    pallas_call x1, Pallas kernels, per_device(): pl.pallas_call(functools.partial(return_kernel, half, capacity, groups, c...  131 us
    unnamed x11, local copies, waits for them, and re-layouts  9.08 us

profile of v3, /device:TPU:0, one launch (start us, length us, event | category | flops | bytes accessed | tf_op | source)
XLA Modules:
  0.0 300.2 jit_solution(2927185261897008028)
XLA Ops:
  0.6 0.7 fusion.3
  1.3 0.1 fusion
  1.5 0.7 select_reduce_fusion
  2.2 0.1 eq.51
  2.3 0.1 copy.22
  2.4 0.1 copy.21
  2.6 0.1 fusion.4
  2.7 0.8 fusion.1
  3.4 0.8 copy.23.sel
  4.2 156.0 %shard_map.110 = (bf16[4,384,1024]{2,1,0:T(8,128)(2,1)}, bf16[4,384,1024]{2,1,0:T(8,128)(2,1)}, bf16[4,384,768]{2,1,0:T(8,128)(2,1)}, bf16[384,768]{1,0:T(8,128)...) custom-call(bf16[2,2,192,128]{3,2,1,0:T(8,128)(2,1)} %copy.23.sel, ...), custom_call_target="tpu_custom_call" | custom-call | tf_op jit(solution)/shard_map/pallas_call | solution.py:391
  160.2 130.8 %shard_map.111 = (bf16[128,4096]{1,0:T(8,128)(2,1)}, bf16[128,4096]{1,0:T(8,128)(2,1)}, bf16[1024,768]{1,0:T(8,128)(2,1)}, bf16[1024,768]{1,0:T(8,128)(2,1)}, bf...) custom-call(bf16[2,2,128,192]{3,2,1,0:T(8,128)(2,1)} %get-tuple-element.32.sel_t, ...), custom_call_target="tpu_custom_call" | custom-call | tf_op jit(solution)/shard_map/pallas_call | solution.py:429
  291.1 0.0 copy-start.2
  291.1 2.4 copy.29
  293.5 0.0 copy-start.1
  293.5 2.4 copy.30
  295.9 0.0 copy-done.2
  295.9 1.1 copy.31
  297.0 0.0 copy-done.1
  297.0 0.0 copy-start
  297.0 1.1 copy.32
  298.2 0.8 copy-done
  299.0 1.1 copy.33
  (5 shorter events, 0.1 us)
Async XLA Ops:
  291.1 4.8 %copy-start.2 = (bf16[1024,768]{1,0:T(8,128)(2,1)S(1)}, bf16[1024,768]{1,0:T(8,128)(2,1)}, u32[]{:S(2)}) copy-start(bf16[1024,768]{1,0:T(8,128)(2,1)} %get-tuple-element.26) | copy-start | bytes 4718596
  293.5 3.6 %copy-start.1 = (bf16[1024,768]{1,0:T(8,128)(2,1)S(1)}, bf16[1024,768]{1,0:T(8,128)(2,1)}, u32[]{:S(2)}) copy-start(bf16[1024,768]{1,0:T(8,128)(2,1)} %get-tuple-element.27) | copy-start | bytes 4718596
  297.0 2.0 copy-start
